TPU v7x, 512 devices: a whole 4x4x16 slice. The times are simulated.
512 devices in a mesh: strip: 128 (over x, z, y_hi), cells: 4 (over y_lo, core).
Axes of the slice: x: 4, y: 4 (y_hi: 2, y_lo: 2; y = y_hi * 2 + y_lo), z: 16, core: 2. Of those that a mesh axis runs over, the one named last changes fastest.
Arguments:
- pin_rows: int32 [2097152], P(('strip', 'cells')), may hold values from 0 to 2
- pin_cols: int32 [2097152], P(('strip', 'cells')), may hold values from 0 to 2558
- pin_fracs: float32 [2, 2097152], P(None, ('strip', 'cells')), may hold values from 0 to 1
- pin_weights: float32 [2097152], P(('strip', 'cells')), may hold values from 0.5 to 1.5
- capacity: int32 [512, 2560], P('strip', 'cells'), may hold values from 1 to 4
- blockage: float32 [512, 2560], P('strip', 'cells'), may hold values from 0 to 0.5
- row_blocks: float32 [20, 128, 128], P('cells'), may hold values from -0.002 to 0.15
- col_blocks: float32 [4, 128, 128], replicated, may hold values from -0.002 to 0.15
Outputs:
- final_density: float32 [512, 2560], P('strip', 'cells')
- pin_velocity: float32 [2, 2097152], P(None, ('strip', 'cells'))
All inputs are finite; a program needn't handle non-finite values.
Results may differ from a plain program's by a relative error of at most 0.0052.
Values may be sent and summed in bfloat16 or wider, within the bound.
A program may use at most 64 MiB of HBM per device.

v0:
```python
import jax
import jax.numpy as jnp
from jax import lax
from jax.sharding import PartitionSpec as P

SWEEPS = 3
STEPS = 2


coupling = 2.0
floor_level = 0.5
highest = lax.Precision.HIGHEST


def padded_2(block, sides, width):
    for axis, dim in sides:
        count = lax.axis_size(axis)
        forward = [(i, i + 1) for i in range(count - 1)]
        backward = [(target, source) for source, target in forward]
        low = lax.ppermute(
            lax.slice_in_dim(block, block.shape[dim] - width, None, axis=dim), axis, forward
        )
        high = lax.ppermute(lax.slice_in_dim(block, 0, width, axis=dim), axis, backward)
        block = jnp.concatenate([low, block, high], axis=dim)
    return block


def along_lines(values):
    padded = jnp.pad(values, ((0, 0), (1, 1)), mode="edge")
    return 2.0 * values - padded[:, :-2] - padded[:, 2:]


def blockwise(residual, blocks):
    leading = residual.shape[0]
    pieces = residual.reshape(leading, blocks.shape[0], blocks.shape[1])
    result = jnp.einsum("rnj,nij->rni", pieces, blocks, precision=highest)
    return result.reshape(leading, blocks.shape[0] * blocks.shape[1])


def line_solve(source, weights, start_iterate, blocks):
    iterate = start_iterate
    for sweep_index in range(SWEEPS):
        residual = source - (weights * iterate + coupling * along_lines(iterate))
        iterate = iterate + blockwise(residual, blocks)
    return iterate


def vertical_rims(values, padded):
    at_first = lax.axis_index("strip") == 0
    at_last = lax.axis_index("strip") == lax.axis_size("strip") - 1
    upper_rim = jnp.where(at_first, values[:1], padded[:1])
    lower_rim = jnp.where(at_last, values[-1:], padded[-1:])
    row_above = jnp.concatenate([upper_rim, values[:-1]], 0)
    row_below = jnp.concatenate([values[1:], lower_rim], 0)
    return (row_above, row_below)


def horizontal_rims(values, padded):
    at_first = lax.axis_index("cells") == 0
    at_last = lax.axis_index("cells") == lax.axis_size("cells") - 1
    left_rim = jnp.where(at_first, values[:, :1], padded[:, :1])
    right_rim = jnp.where(at_last, values[:, -1:], padded[:, -1:])
    left_cells = jnp.concatenate([left_rim, values[:, :-1]], 1)
    right_cells = jnp.concatenate([values[:, 1:], right_rim], 1)
    return (left_cells, right_cells)


def row_lines(values):
    padded = padded_2(values, (("cells", 1),), 1)
    left_cells, right_cells = horizontal_rims(values, padded)
    return 2.0 * values - left_cells - right_cells


def row_solve(source, weights, start_iterate, blocks):
    iterate = start_iterate
    for sweep_index in range(SWEEPS):
        residual = source - (weights * iterate + coupling * row_lines(iterate))
        iterate = iterate + blockwise(residual, blocks)
    return iterate


def pin_tables(block_rows, block_cols, row_near, row_far, col_near, col_far, rows_dev, hi_count):
    block_size = block_rows.shape[0]
    zero_value = jnp.zeros((), jnp.bfloat16)
    row_index = lax.broadcasted_iota(jnp.int32, (block_size, rows_dev), 1)
    row_table = jnp.where(
        row_index == block_rows[:, None], row_near[:, None], zero_value
    ) + jnp.where(row_index == block_rows[:, None] + 1, row_far[:, None], zero_value)
    high_index = lax.broadcasted_iota(jnp.int32, (block_size, 1, hi_count), 2)
    low_index = lax.broadcasted_iota(jnp.int32, (block_size, 128), 1)
    bin_tables = []
    lane_tables = []
    for offset, factor in ((0, col_near), (1, col_far)):
        column = block_cols + offset
        high_part = column // 128
        low_part = column - high_part * 128
        chosen = (high_index == high_part[:, None, None]).astype(jnp.bfloat16)
        bin_tables.append((row_table[:, :, None] * chosen).reshape(block_size, rows_dev * hi_count))
        lane_tables.append(jnp.where(low_index == low_part[:, None], factor[:, None], zero_value))
    return (jnp.concatenate(bin_tables, 0), jnp.concatenate(lane_tables, 0))


def pin_factors(pin_rows, pin_cols, row_near, row_far, col_near, col_far):
    block_size = min(2048, pin_rows.shape[0])
    return (
        block_size,
        tuple(
            (
                item.reshape(-1, block_size)
                for item in (pin_rows, pin_cols, row_near, row_far, col_near, col_far)
            )
        ),
    )


def splat(pin_rows, pin_cols, pin_fracs, pin_weights, rows_dev, hi_count):
    near_y = 1.0 - pin_fracs[0]
    near_x = 1.0 - pin_fracs[1]
    block_size, pieces = pin_factors(
        pin_rows,
        pin_cols,
        (pin_weights * near_y).astype(jnp.bfloat16),
        (pin_weights * pin_fracs[0]).astype(jnp.bfloat16),
        near_x.astype(jnp.bfloat16),
        pin_fracs[1].astype(jnp.bfloat16),
    )

    def add_block(total, block):
        bins, lane_table = pin_tables(
            block[0], block[1], block[2], block[3], block[4], block[5], rows_dev, hi_count
        )
        part_sum = lax.dot_general(
            bins, lane_table, (((0,), (0,)), ((), ())), preferred_element_type=jnp.float32
        )
        return (total + part_sum, None)

    total, unused = lax.scan(add_block, jnp.zeros((rows_dev * hi_count, 128), jnp.float32), pieces)
    return total.reshape(rows_dev, hi_count * 128)


def interpolate(pin_rows, pin_cols, pin_fracs, velocity_y, velocity_x, rows_dev, hi_count):
    stacked = jnp.concatenate(
        [
            velocity_y.reshape(rows_dev * hi_count, 128),
            velocity_x.reshape(rows_dev * hi_count, 128),
        ],
        1,
    )
    npins = pin_rows.shape[0]
    block_size, pieces = pin_factors(
        pin_rows,
        pin_cols,
        (1.0 - pin_fracs[0]).astype(jnp.bfloat16),
        pin_fracs[0].astype(jnp.bfloat16),
        (1.0 - pin_fracs[1]).astype(jnp.bfloat16),
        pin_fracs[1].astype(jnp.bfloat16),
    )

    def one_block(carry, block):
        bins, lane_table = pin_tables(
            block[0], block[1], block[2], block[3], block[4], block[5], rows_dev, hi_count
        )
        sampled = jnp.dot(bins, stacked, preferred_element_type=jnp.float32)
        lane_values = lane_table.astype(jnp.float32)
        both_y = jnp.sum(sampled[:, :128] * lane_values, axis=1)
        both_x = jnp.sum(sampled[:, 128:] * lane_values, axis=1)
        result = jnp.stack(
            [both_y[:block_size] + both_y[block_size:], both_x[:block_size] + both_x[block_size:]]
        )
        return (carry, result)

    unused, outputs = lax.scan(one_block, jnp.zeros((), jnp.float32), pieces)
    return jnp.transpose(outputs, (1, 0, 2)).reshape(2, npins)


def velocity_of(centre, left_cells, right_cells, row_above, row_below):
    scale = jnp.maximum(centre, floor_level)
    velocity_x = (-(0.5 * (right_cells - left_cells)) / scale).astype(jnp.bfloat16)
    velocity_y = (-(0.5 * (row_below - row_above)) / scale).astype(jnp.bfloat16)
    return (velocity_y, velocity_x)


def to_rows_middle(source_col, current_col):
    source_back, current_back = (
        lax.all_to_all(source_col, "strip", split_axis=1, concat_axis=0, tiled=True),
        lax.all_to_all(current_col, "strip", split_axis=1, concat_axis=0, tiled=True),
    )
    return (source_back.T, current_back.T)


def local(pin_rows, pin_cols, pin_fracs, pin_weights, capacity, blockage, row_blocks, col_blocks):
    rows_dev, cols_dev = capacity.shape
    hi_count = cols_dev * lax.axis_size("cells") // 128
    cap_weight = capacity.astype(jnp.float32) * (1.0 - blockage)
    partial_value = splat(pin_rows, pin_cols, pin_fracs, pin_weights, rows_dev, hi_count)
    whole = lax.psum(partial_value, "cells")
    density = lax.dynamic_slice_in_dim(whole, lax.axis_index("cells") * cols_dev, cols_dev, 1)
    current = density / cap_weight
    row_above, row_below = vertical_rims(current, padded_2(current, (("strip", 0),), 1))
    source = cap_weight * current - coupling * (2.0 * current - row_above - row_below)
    column_weight = cap_weight.T
    for step_index in range(STEPS):
        current = row_solve(source, cap_weight, current, row_blocks)
        middle = cap_weight * current - coupling * row_lines(current)
        if step_index == 0:
            middle_col, current_col, column_weight = (
                lax.all_to_all(middle.T, "strip", split_axis=0, concat_axis=1, tiled=True),
                lax.all_to_all(current.T, "strip", split_axis=0, concat_axis=1, tiled=True),
                lax.all_to_all(cap_weight.T, "strip", split_axis=0, concat_axis=1, tiled=True),
            )
        else:
            middle_col, current_col = (
                lax.all_to_all(middle.T, "strip", split_axis=0, concat_axis=1, tiled=True),
                lax.all_to_all(current.T, "strip", split_axis=0, concat_axis=1, tiled=True),
            )
        current_col = line_solve(middle_col, column_weight, current_col, col_blocks)
        if step_index + 1 < STEPS:
            source_col = column_weight * current_col - coupling * along_lines(current_col)
            source, current = to_rows_middle(source_col, current_col)
        else:
            current = lax.all_to_all(
                current_col, "strip", split_axis=1, concat_axis=0, tiled=True
            ).T
    padded = padded_2(current, (("strip", 0),), 1)
    row_above, row_below = vertical_rims(current, padded)
    extended = jnp.concatenate([row_above[:1], current, row_below[-1:]], 0)
    strip_field = lax.all_gather(extended, "cells", axis=1, tiled=True)
    centre = strip_field[1:-1]
    padded_cols = jnp.pad(centre, ((0, 0), (1, 1)), mode="edge")
    velocity_y, velocity_x = velocity_of(
        centre, padded_cols[:, :-2], padded_cols[:, 2:], strip_field[:-2], strip_field[2:]
    )
    pin_velocity = interpolate(
        pin_rows, pin_cols, pin_fracs, velocity_y, velocity_x, rows_dev, hi_count
    )
    return (current, pin_velocity)


def solution(mesh):
    placed = (
        P(("strip", "cells")),
        P(("strip", "cells")),
        P(None, ("strip", "cells")),
        P(("strip", "cells")),
        P("strip", "cells"),
        P("strip", "cells"),
        P("cells", None, None),
        P(),
    )
    return jax.shard_map(
        local,
        mesh=mesh,
        in_specs=placed,
        out_specs=(P("strip", "cells"), P(None, ("strip", "cells"))),
        check_vma=False,
    )
```

profile of v0, /device:TPU:1, one launch (start us, length us, event | category | flops | bytes accessed | tf_op | source)
XLA Modules:
  0.0 360.2 jit_solution(1217124088684022268)
XLA Ops:
  4.7 4.6 %while.28 = (s32[]{:T(128)}, f32[80,128]{1,0:T(8,128)S(1)}, s32[2,2048]{1,0:T(2,128)S(1)}, bf16[2,2048]{1,0:T(2,128)(2,1)S(1)}, bf16[2,2048]{1,0:T(2,128)(2,1)S(...) while((s32[]{:T(128)}, f32[80,128]{1,0:T(8,128)S(1)}, ...), condition=%wide.region_1.2_spmd.clone, body=%wide.region_0.1_spmd.clone.sunk | while | flops 88993792 | bytes 5349499 | solution.py:137
  9.4 16.6 %psum.7 = f32[4,2560]{1,0:T(4,128)S(1)} all-reduce(f32[4,2560]{1,0:T(4,128)S(1)} %reshape.768), channel_id=1, replica_groups=mesh['strip'=128,'cells'=4] {'cells'}, use_global_device_ids=true, to_apply=%region_2.3 | all-reduce | flops 10240 | bytes 81920 | tf_op jit(solution)/shard_map/psum | solution.py:196
  34.1 23.2 %all-to-all-start.2 = ((f32[128,5,4]{1,2,0:T(4,128)}), f32[128,5,4]{1,2,0:T(4,128)S(1)}, u32[]{:S(2)}, u32[]{:S(2)}) async-start(f32[128,5,4]{1,2,0:T(4,128)} %copy.55), calls=%async_computation.2 | async-start | bytes 524288 | tf_op jit(solution)/shard_map/all_to_all | solution.py:209
  58.4 3.3 collective-permute-start.4
  63.7 3.3 collective-permute-done.5
  69.7 2.4 collective-permute-start.7
  72.2 2.8 collective-permute-done.7
  77.7 2.4 collective-permute-start.9
  82.7 18.7 %all-to-all-start = ((f32[128,5,4]{1,2,0:T(4,128)}), f32[128,5,4]{1,2,0:T(4,128)S(1)}, u32[]{:S(2)}, u32[]{:S(2)}) async-start(f32[128,5,4]{1,2,0:T(4,128)} %copy.51), calls=%async_computation | async-start | bytes 524288 | tf_op jit(solution)/shard_map/all_to_all | solution.py:208
  102.7 22.7 %all-to-all-done = f32[128,5,4]{1,2,0:T(4,128)S(1)} async-done(((f32[128,5,4]{1,2,0:T(4,128)}), f32[128,5,4]{1,2,0:T(4,128)S(1)}, u32[]{:S(2)}, u32[]{:S(2)}) %all-to-all-start) | async-done | bytes 10272 | tf_op jit(solution)/shard_map/all_to_all | solution.py:208
  125.4 6.3 %all-to-all-start.1 = ((f32[128,5,4]{1,2,0:T(4,128)}), f32[128,5,4]{1,2,0:T(4,128)S(1)}, u32[]{:S(2)}, u32[]{:S(2)}) async-start(f32[128,5,4]{1,2,0:T(4,128)} %copy.53), calls=%async_computation.1 | async-start | bytes 524288 | tf_op jit(solution)/shard_map/all_to_all | solution.py:207
  133.1 21.1 %all-to-all-done.1 = f32[128,5,4]{1,2,0:T(4,128)S(1)} async-done(((f32[128,5,4]{1,2,0:T(4,128)}), f32[128,5,4]{1,2,0:T(4,128)S(1)}, u32[]{:S(2)}, u32[]{:S(2)}) %all-to-all-start.1) | async-done | bytes 10272 | tf_op jit(solution)/shard_map/all_to_all | solution.py:207
  158.9 7.5 %all-to-all-start.3 = ((f32[5,128,4]{0,2,1:T(4,128)}), f32[5,128,4]{0,2,1:T(4,128)S(1)}, u32[]{:S(2)}, u32[]{:S(2)}) async-start(f32[5,128,4]{0,2,1:T(4,128)} %copy.63), calls=%async_computation.3 | async-start | bytes 524288 | tf_op jit(solution)/shard_map/all_to_all | solution.py:186
  167.4 19.8 %all-to-all-done.3 = f32[5,128,4]{0,2,1:T(4,128)S(1)} async-done(((f32[5,128,4]{0,2,1:T(4,128)}), f32[5,128,4]{0,2,1:T(4,128)S(1)}, u32[]{:S(2)}, u32[]{:S(2)}) %all-to-all-start.3) | async-done | bytes 10272 | tf_op jit(solution)/shard_map/all_to_all | solution.py:186
  187.1 8.8 %all-to-all-start.4 = ((f32[5,128,4]{0,2,1:T(4,128)}), f32[5,128,4]{0,2,1:T(4,128)S(1)}, u32[]{:S(2)}, u32[]{:S(2)}) async-start(f32[5,128,4]{0,2,1:T(4,128)} %bitcast.36), calls=%async_computation.4 | async-start | bytes 524288 | tf_op jit(solution)/shard_map/all_to_all | solution.py:185
  196.3 19.9 %all-to-all-done.4 = f32[5,128,4]{0,2,1:T(4,128)S(1)} async-done(((f32[5,128,4]{0,2,1:T(4,128)}), f32[5,128,4]{0,2,1:T(4,128)S(1)}, u32[]{:S(2)}, u32[]{:S(2)}) %all-to-all-start.4) | async-done | bytes 10272 | tf_op jit(solution)/shard_map/all_to_all | solution.py:185
  216.4 3.5 collective-permute-start.10
  220.0 5.2 %collective-permute-start.11 = (f32[4,1]{1,0:T(4,128)S(1)}, f32[4,1]{1,0:T(4,128)S(1)}, u32[]{:S(2)}, u32[]{:S(2)}) collective-permute-start(f32[4,1]{1,0:T(4,128)S(1)} %get-tuple-element.409), channel_id=1, source_target_pairs={{1,0},{2,1},{3,2},{5,4},{6,5},{7,6},{9,8},{10,9},{11,10},{13,12},{... | collective-permute-start | bytes 56 | tf_op jit(solution)/shard_map/ppermute | solution.py:23
  228.8 2.4 collective-permute-start.13
  231.2 2.5 collective-permute-done.13
  238.9 2.5 collective-permute-done.15
  243.4 6.6 %all-to-all-start.5 = ((f32[128,5,4]{1,2,0:T(4,128)}), f32[128,5,4]{1,2,0:T(4,128)S(1)}, u32[]{:S(2)}, u32[]{:S(2)}) async-start(f32[128,5,4]{1,2,0:T(4,128)} %copy.70), calls=%async_computation.5 | async-start | bytes 524288 | tf_op jit(solution)/shard_map/all_to_all | solution.py:214
  251.9 2.4 collective-permute-start.17
  254.4 2.8 collective-permute-done.17
  258.4 15.6 %all-to-all-done.5 = f32[128,5,4]{1,2,0:T(4,128)S(1)} async-done(((f32[128,5,4]{1,2,0:T(4,128)}), f32[128,5,4]{1,2,0:T(4,128)S(1)}, u32[]{:S(2)}, u32[]{:S(2)}) %all-to-all-start.5) | async-done | bytes 10272 | tf_op jit(solution)/shard_map/all_to_all | solution.py:214
  274.0 6.4 %all-to-all-start.6 = ((f32[128,5,4]{1,2,0:T(4,128)}), f32[128,5,4]{1,2,0:T(4,128)S(1)}, u32[]{:S(2)}, u32[]{:S(2)}) async-start(f32[128,5,4]{1,2,0:T(4,128)} %copy.72), calls=%async_computation.6 | async-start | bytes 524288 | tf_op jit(solution)/shard_map/all_to_all | solution.py:213
  281.8 21.3 %all-to-all-done.6 = f32[128,5,4]{1,2,0:T(4,128)S(1)} async-done(((f32[128,5,4]{1,2,0:T(4,128)}), f32[128,5,4]{1,2,0:T(4,128)S(1)}, u32[]{:S(2)}, u32[]{:S(2)}) %all-to-all-start.6) | async-done | bytes 10272 | tf_op jit(solution)/shard_map/all_to_all | solution.py:213
  307.0 28.3 %all_to_all.146 = f32[5,128,4]{0,2,1:T(4,128)S(1)} all-to-all(f32[5,128,4]{0,2,1:T(4,128)S(1)} %copy.80), channel_id=1, replica_groups=mesh['strip'=128,'cells'=4] {'strip'}, dimensions={1} | all-to-all | bytes 20480 | tf_op jit(solution)/shard_map/all_to_all | solution.py:221
  335.5 3.4 collective-permute-start.18
  340.2 4.5 %collective-permute-done.19 = f32[1,640]{1,0:T(1,128)S(1)} collective-permute-done((f32[1,640]{1,0:T(1,128)S(1)}, f32[1,640]{1,0:T(1,128)S(1)}, u32[]{:S(2)}, u32[]{:S(2)}) %collective-permute-start.19) | collective-permute-done | bytes 2592 | tf_op jit(solution)/shard_map/ppermute | solution.py:23
  344.8 10.5 %all_gather.3 = f32[6,2560]{1,0:T(8,128)S(1)} all-gather(f32[6,640]{1,0:T(8,128)S(1)} %pad_maximum_fusion.4), channel_id=1, replica_groups=mesh['strip'=128,'cells'=4] {'cells'}, dimensions={1}, use_global_device_ids=true | all-gather | bytes 76800 | tf_op jit(solution)/shard_map/all_gather | solution.py:227
  355.5 4.1 %while.27 = (s32[]{:T(128)}, f32[2,2,2048]{2,1,0:T(2,128)S(1)}, s32[2,2048]{1,0:T(2,128)S(1)}, bf16[2,2048]{1,0:T(2,128)(2,1)S(1)}, bf16[2,2048]{1,0:T(2,128)(2,...) while((s32[]{:T(128)}, f32[2,2,2048]{2,1,0:T(2,128)S(1)}, ...), condition=%wide.region_6.7_spmd, body=%wide.region_3.6_spmd.sunk | while | flops 174956544 | bytes 13811829 | solution.py:172
  (217 shorter events, 61.9 us)
Async XLA Ops:
  0.6 56.9 %copy-start = (f32[5,128,128]{2,1,0:T(8,128)S(1)}, f32[5,128,128]{2,1,0:T(8,128)}, u32[]{:S(2)}) copy-start(f32[5,128,128]{2,1,0:T(8,128)} %param.18) | copy-start | bytes 983044
  4.7 21.3 %copy-start.3 = (f32[4,640]{1,0:T(4,128)S(1)}, f32[4,640]{1,0:T(4,128)}, u32[]{:S(2)}) copy-start(f32[4,640]{1,0:T(4,128)} %param.17) | copy-start | bytes 30724
  4.7 21.3 %copy-start.4 = (s32[4,640]{1,0:T(4,128)S(1)}, s32[4,640]{1,0:T(4,128)}, u32[]{:S(2)}) copy-start(s32[4,640]{1,0:T(4,128)} %param.16) | copy-start | bytes 30724
  26.0 31.5 %collective-permute-start = (f32[1,640]{1,0:T(1,128)S(1)}, f32[1,640]{1,0:T(1,128)S(1)}, u32[]{:S(2)}, u32[]{:S(2)}) collective-permute-start(f32[1,640]{1,0:T(1,128)S(1)} %get-tuple-element.440), channel_id=1, source_target_pairs={{0,4},{4,8},{8,12},{12,16},{16,20},{20,24},{24,28},{28,32},{32,36}... | collective-permute-start | bytes 7688 | tf_op jit(solution)/shard_map/ppermute | solution.py:20
  27.3 30.2 %collective-permute-start.1 = (f32[1,640]{1,0:T(1,128)S(1)}, f32[1,640]{1,0:T(1,128)S(1)}, u32[]{:S(2)}, u32[]{:S(2)}) collective-permute-start(f32[1,640]{1,0:T(1,128)S(1)} %get-tuple-element.439), channel_id=1, source_target_pairs={{4,0},{8,4},{12,8},{16,12},{20,16},{24,20},{28,24},{32,28},{36,32}... | collective-permute-start | bytes 7688 | tf_op jit(solution)/shard_map/ppermute | solution.py:23
  28.7 28.8 %collective-permute-start.2 = (f32[4,1]{1,0:T(4,128)S(1)}, f32[4,1]{1,0:T(4,128)S(1)}, u32[]{:S(2)}, u32[]{:S(2)}) collective-permute-start(f32[4,1]{1,0:T(4,128)S(1)} %get-tuple-element.434), channel_id=1, source_target_pairs={{0,1},{1,2},{2,3},{4,5},{5,6},{6,7},{8,9},{9,10},{10,11},{12,13},{... | collective-permute-start | bytes 56 | tf_op jit(solution)/shard_map/ppermute | solution.py:20
  30.8 26.7 %collective-permute-start.3 = (f32[4,1]{1,0:T(4,128)S(1)}, f32[4,1]{1,0:T(4,128)S(1)}, u32[]{:S(2)}, u32[]{:S(2)}) collective-permute-start(f32[4,1]{1,0:T(4,128)S(1)} %get-tuple-element.433), channel_id=1, source_target_pairs={{1,0},{2,1},{3,2},{5,4},{6,5},{7,6},{9,8},{10,9},{11,10},{13,12},{... | collective-permute-start | bytes 56 | tf_op jit(solution)/shard_map/ppermute | solution.py:23
  34.1 48.6 %all-to-all-start.2 = ((f32[128,5,4]{1,2,0:T(4,128)}), f32[128,5,4]{1,2,0:T(4,128)S(1)}, u32[]{:S(2)}, u32[]{:S(2)}) async-start(f32[128,5,4]{1,2,0:T(4,128)} %copy.55), calls=%async_computation.2 | async-start | bytes 524288 | tf_op jit(solution)/shard_map/all_to_all | solution.py:209
  58.4 5.3 %collective-permute-start.4 = (f32[4,1]{1,0:T(4,128)S(1)}, f32[4,1]{1,0:T(4,128)S(1)}, u32[]{:S(2)}, u32[]{:S(2)}) collective-permute-start(f32[4,1]{1,0:T(4,128)S(1)} %get-tuple-element.428), channel_id=1, source_target_pairs={{0,1},{1,2},{2,3},{4,5},{5,6},{6,7},{8,9},{9,10},{10,11},{12,13},{... | collective-permute-start | bytes 56 | tf_op jit(solution)/shard_map/ppermute | solution.py:20
  61.7 5.2 %collective-permute-start.5 = (f32[4,1]{1,0:T(4,128)S(1)}, f32[4,1]{1,0:T(4,128)S(1)}, u32[]{:S(2)}, u32[]{:S(2)}) collective-permute-start(f32[4,1]{1,0:T(4,128)S(1)} %get-tuple-element.427), channel_id=1, source_target_pairs={{1,0},{2,1},{3,2},{5,4},{6,5},{7,6},{9,8},{10,9},{11,10},{13,12},{... | collective-permute-start | bytes 56 | tf_op jit(solution)/shard_map/ppermute | solution.py:23
  67.8 4.3 %collective-permute-start.6 = (f32[4,1]{1,0:T(4,128)S(1)}, f32[4,1]{1,0:T(4,128)S(1)}, u32[]{:S(2)}, u32[]{:S(2)}) collective-permute-start(f32[4,1]{1,0:T(4,128)S(1)} %get-tuple-element.422), channel_id=1, source_target_pairs={{0,1},{1,2},{2,3},{4,5},{5,6},{6,7},{8,9},{9,10},{10,11},{12,13},{... | collective-permute-start | bytes 56 | tf_op jit(solution)/shard_map/ppermute | solution.py:20
  69.7 5.2 %collective-permute-start.7 = (f32[4,1]{1,0:T(4,128)S(1)}, f32[4,1]{1,0:T(4,128)S(1)}, u32[]{:S(2)}, u32[]{:S(2)}) collective-permute-start(f32[4,1]{1,0:T(4,128)S(1)} %get-tuple-element.421), channel_id=1, source_target_pairs={{1,0},{2,1},{3,2},{5,4},{6,5},{7,6},{9,8},{10,9},{11,10},{13,12},{... | collective-permute-start | bytes 56 | tf_op jit(solution)/shard_map/ppermute | solution.py:23
  75.8 5.5 %collective-permute-start.8 = (f32[4,1]{1,0:T(4,128)S(1)}, f32[4,1]{1,0:T(4,128)S(1)}, u32[]{:S(2)}, u32[]{:S(2)}) collective-permute-start(f32[4,1]{1,0:T(4,128)S(1)} %get-tuple-element.416), channel_id=1, source_target_pairs={{0,1},{1,2},{2,3},{4,5},{5,6},{6,7},{8,9},{9,10},{10,11},{12,13},{... | collective-permute-start | bytes 56 | tf_op jit(solution)/shard_map/ppermute | solution.py:20
  77.7 4.9 %collective-permute-start.9 = (f32[4,1]{1,0:T(4,128)S(1)}, f32[4,1]{1,0:T(4,128)S(1)}, u32[]{:S(2)}, u32[]{:S(2)}) collective-permute-start(f32[4,1]{1,0:T(4,128)S(1)} %get-tuple-element.415), channel_id=1, source_target_pairs={{1,0},{2,1},{3,2},{5,4},{6,5},{7,6},{9,8},{10,9},{11,10},{13,12},{... | collective-permute-start | bytes 56 | tf_op jit(solution)/shard_map/ppermute | solution.py:23
  80.2 74.1 %copy-start.1 = (f32[4,128,128]{2,1,0:T(8,128)S(1)}, f32[4,128,128]{2,1,0:T(8,128)}, u32[]{:S(2)}) copy-start(f32[4,128,128]{2,1,0:T(8,128)} %param.19) | copy-start | bytes 786436
  82.7 42.7 %all-to-all-start = ((f32[128,5,4]{1,2,0:T(4,128)}), f32[128,5,4]{1,2,0:T(4,128)S(1)}, u32[]{:S(2)}, u32[]{:S(2)}) async-start(f32[128,5,4]{1,2,0:T(4,128)} %copy.51), calls=%async_computation | async-start | bytes 524288 | tf_op jit(solution)/shard_map/all_to_all | solution.py:208
  125.4 28.7 %all-to-all-start.1 = ((f32[128,5,4]{1,2,0:T(4,128)}), f32[128,5,4]{1,2,0:T(4,128)S(1)}, u32[]{:S(2)}, u32[]{:S(2)}) async-start(f32[128,5,4]{1,2,0:T(4,128)} %copy.53), calls=%async_computation.1 | async-start | bytes 524288 | tf_op jit(solution)/shard_map/all_to_all | solution.py:207
  158.9 28.2 %all-to-all-start.3 = ((f32[5,128,4]{0,2,1:T(4,128)}), f32[5,128,4]{0,2,1:T(4,128)S(1)}, u32[]{:S(2)}, u32[]{:S(2)}) async-start(f32[5,128,4]{0,2,1:T(4,128)} %copy.63), calls=%async_computation.3 | async-start | bytes 524288 | tf_op jit(solution)/shard_map/all_to_all | solution.py:186
  187.1 29.1 %all-to-all-start.4 = ((f32[5,128,4]{0,2,1:T(4,128)}), f32[5,128,4]{0,2,1:T(4,128)S(1)}, u32[]{:S(2)}, u32[]{:S(2)}) async-start(f32[5,128,4]{0,2,1:T(4,128)} %bitcast.36), calls=%async_computation.4 | async-start | bytes 524288 | tf_op jit(solution)/shard_map/all_to_all | solution.py:185
  216.4 8.7 %collective-permute-start.10 = (f32[4,1]{1,0:T(4,128)S(1)}, f32[4,1]{1,0:T(4,128)S(1)}, u32[]{:S(2)}, u32[]{:S(2)}) collective-permute-start(f32[4,1]{1,0:T(4,128)S(1)} %get-tuple-element.410), channel_id=1, source_target_pairs={{0,1},{1,2},{2,3},{4,5},{5,6},{6,7},{8,9},{9,10},{10,11},{12,13},{... | collective-permute-start | bytes 56 | tf_op jit(solution)/shard_map/ppermute | solution.py:20
  220.0 6.0 %collective-permute-start.11 = (f32[4,1]{1,0:T(4,128)S(1)}, f32[4,1]{1,0:T(4,128)S(1)}, u32[]{:S(2)}, u32[]{:S(2)}) collective-permute-start(f32[4,1]{1,0:T(4,128)S(1)} %get-tuple-element.409), channel_id=1, source_target_pairs={{1,0},{2,1},{3,2},{5,4},{6,5},{7,6},{9,8},{10,9},{11,10},{13,12},{... | collective-permute-start | bytes 56 | tf_op jit(solution)/shard_map/ppermute | solution.py:23
  226.8 4.3 %collective-permute-start.12 = (f32[4,1]{1,0:T(4,128)S(1)}, f32[4,1]{1,0:T(4,128)S(1)}, u32[]{:S(2)}, u32[]{:S(2)}) collective-permute-start(f32[4,1]{1,0:T(4,128)S(1)} %get-tuple-element.404), channel_id=1, source_target_pairs={{0,1},{1,2},{2,3},{4,5},{5,6},{6,7},{8,9},{9,10},{10,11},{12,13},{... | collective-permute-start | bytes 56 | tf_op jit(solution)/shard_map/ppermute | solution.py:20
  228.8 4.9 %collective-permute-start.13 = (f32[4,1]{1,0:T(4,128)S(1)}, f32[4,1]{1,0:T(4,128)S(1)}, u32[]{:S(2)}, u32[]{:S(2)}) collective-permute-start(f32[4,1]{1,0:T(4,128)S(1)} %get-tuple-element.403), channel_id=1, source_target_pairs={{1,0},{2,1},{3,2},{5,4},{6,5},{7,6},{9,8},{10,9},{11,10},{13,12},{... | collective-permute-start | bytes 56 | tf_op jit(solution)/shard_map/ppermute | solution.py:23
  234.5 4.3 %collective-permute-start.14 = (f32[4,1]{1,0:T(4,128)S(1)}, f32[4,1]{1,0:T(4,128)S(1)}, u32[]{:S(2)}, u32[]{:S(2)}) collective-permute-start(f32[4,1]{1,0:T(4,128)S(1)} %get-tuple-element.398), channel_id=1, source_target_pairs={{0,1},{1,2},{2,3},{4,5},{5,6},{6,7},{8,9},{9,10},{10,11},{12,13},{... | collective-permute-start | bytes 56 | tf_op jit(solution)/shard_map/ppermute | solution.py:20
  236.5 4.9 %collective-permute-start.15 = (f32[4,1]{1,0:T(4,128)S(1)}, f32[4,1]{1,0:T(4,128)S(1)}, u32[]{:S(2)}, u32[]{:S(2)}) collective-permute-start(f32[4,1]{1,0:T(4,128)S(1)} %get-tuple-element.397), channel_id=1, source_target_pairs={{1,0},{2,1},{3,2},{5,4},{6,5},{7,6},{9,8},{10,9},{11,10},{13,12},{... | collective-permute-start | bytes 56 | tf_op jit(solution)/shard_map/ppermute | solution.py:23
  243.4 30.6 %all-to-all-start.5 = ((f32[128,5,4]{1,2,0:T(4,128)}), f32[128,5,4]{1,2,0:T(4,128)S(1)}, u32[]{:S(2)}, u32[]{:S(2)}) async-start(f32[128,5,4]{1,2,0:T(4,128)} %copy.70), calls=%async_computation.5 | async-start | bytes 524288 | tf_op jit(solution)/shard_map/all_to_all | solution.py:214
  250.0 4.3 %collective-permute-start.16 = (f32[4,1]{1,0:T(4,128)S(1)}, f32[4,1]{1,0:T(4,128)S(1)}, u32[]{:S(2)}, u32[]{:S(2)}) collective-permute-start(f32[4,1]{1,0:T(4,128)S(1)} %get-tuple-element.392), channel_id=1, source_target_pairs={{0,1},{1,2},{2,3},{4,5},{5,6},{6,7},{8,9},{9,10},{10,11},{12,13},{... | collective-permute-start | bytes 56 | tf_op jit(solution)/shard_map/ppermute | solution.py:20
  251.9 5.2 %collective-permute-start.17 = (f32[4,1]{1,0:T(4,128)S(1)}, f32[4,1]{1,0:T(4,128)S(1)}, u32[]{:S(2)}, u32[]{:S(2)}) collective-permute-start(f32[4,1]{1,0:T(4,128)S(1)} %get-tuple-element.391), channel_id=1, source_target_pairs={{1,0},{2,1},{3,2},{5,4},{6,5},{7,6},{9,8},{10,9},{11,10},{13,12},{... | collective-permute-start | bytes 56 | tf_op jit(solution)/shard_map/ppermute | solution.py:23
  274.0 29.0 %all-to-all-start.6 = ((f32[128,5,4]{1,2,0:T(4,128)}), f32[128,5,4]{1,2,0:T(4,128)S(1)}, u32[]{:S(2)}, u32[]{:S(2)}) async-start(f32[128,5,4]{1,2,0:T(4,128)} %copy.72), calls=%async_computation.6 | async-start | bytes 524288 | tf_op jit(solution)/shard_map/all_to_all | solution.py:213
  335.5 20.0 %copy-start.2 = (f32[640,4]{0,1:T(4,128)}, f32[640,4]{0,1:T(4,128)S(1)}, u32[]{:S(2)}) copy-start(f32[640,4]{0,1:T(4,128)S(1)} %all_to_all.137) | copy-start | bytes 30724
  335.5 4.7 %collective-permute-start.18 = (f32[1,640]{1,0:T(1,128)S(1)}, f32[1,640]{1,0:T(1,128)S(1)}, u32[]{:S(2)}, u32[]{:S(2)}) collective-permute-start(f32[1,640]{1,0:T(1,128)S(1)} %get-tuple-element.385), channel_id=1, source_target_pairs={{0,4},{4,8},{8,12},{12,16},{16,20},{20,24},{24,28},{28,32},{32,36}... | collective-permute-start | bytes 7688 | tf_op jit(solution)/shard_map/ppermute | solution.py:20
  338.9 5.8 %collective-permute-start.19 = (f32[1,640]{1,0:T(1,128)S(1)}, f32[1,640]{1,0:T(1,128)S(1)}, u32[]{:S(2)}, u32[]{:S(2)}) collective-permute-start(f32[1,640]{1,0:T(1,128)S(1)} %get-tuple-element.386), channel_id=1, source_target_pairs={{4,0},{8,4},{12,8},{16,12},{20,16},{24,20},{28,24},{32,28},{36,32}... | collective-permute-start | bytes 7688 | tf_op jit(solution)/shard_map/ppermute | solution.py:23
  (1 other events, 0.6 us)
where the time goes:
time: 362 us; the launch traced here: 360 us
  waiting for transfers between devices  141 us (39%)
  starting transfers between devices  125 us (35%)
  blocking collectives  55.3 us (15%)
  local copies, waits for them, and re-layouts  20.3 us (6%)
  matrix products  9.52 us (3%)
  other arithmetic  7.8 us (2%)
    all_to_all x2, waiting for transfers between devices, local(): lax.all_to_all(middle.T, 'strip', split_axis=0, concat_axis=1, tiled=True)  42.3 us
    all_to_all x2, waiting for transfers between devices, local(): lax.all_to_all(current.T, 'strip', split_axis=0, concat_axis=1, tiled=True)  38.4 us
    all_to_all x1, blocking collectives, local(): lax.all_to_all(current_col, 'strip', split_axis=1, concat_axis=0, tiled=T...  28.3 us
    all_to_all x2, starting transfers between devices, local(): lax.all_to_all(current.T, 'strip', split_axis=0, concat_axis=1, tiled=True)  25.3 us
    ppermute x10, starting transfers between devices, padded_2(): lax.ppermute(lax.slice_in_dim(block, 0, width, axis=dim), axis, backward)  23.9 us
    ppermute x10, starting transfers between devices, padded_2(): lax.ppermute(lax.slice_in_dim(block, block.shape[dim] - width, None, axis...  23.3 us
    all_to_all x1, starting transfers between devices, local(): lax.all_to_all(cap_weight.T, 'strip', split_axis=0, concat_axis=1, tiled=...  23.2 us
    ppermute x10, waiting for transfers between devices, padded_2(): lax.ppermute(lax.slice_in_dim(block, 0, width, axis=dim), axis, backward)  20.5 us
  transfers between devices with their start and end apart: 27, of which 14 were waited for; matrix products, arithmetic and copies ran while one was open for 3% of the time, Pallas kernels for 0%

commit v1 on v0

v1 whole, which is shorter than its diff:
```python
import functools

import jax
import jax.numpy as jnp
from jax import lax
from jax.experimental import pallas as pl
from jax.experimental.pallas import tpu as pltpu
from jax.sharding import PartitionSpec as P

SWEEPS = 3
STEPS = 2
coupling = 2.0
floor_level = 0.5
f32 = jnp.float32
bf16 = jnp.bfloat16


def exact_parts(values):
    high = values.astype(bf16)
    return high, (values - high.astype(f32)).astype(bf16)


def row_product(values, high_ref, low_ref):
    pieces = []
    for n in range(high_ref.shape[0]):
        high, low = exact_parts(values[:, 128 * n : 128 * (n + 1)])
        dims = (((1,), (1,)), ((), ()))
        dot = functools.partial(lax.dot_general, dimension_numbers=dims, preferred_element_type=f32)
        pieces.append(
            dot(high, high_ref[n]) + (dot(low, high_ref[n]) + dot(high, low_ref[n]))
        )
    return jnp.concatenate(pieces, axis=1)


def col_product(matrix, values):
    high, low = exact_parts(values)
    dot = functools.partial(jnp.dot, preferred_element_type=f32)
    return dot(matrix[0], high) + (dot(matrix[0], low) + dot(matrix[1], high))


def adi_kernel(
    sizes,
    part_ref,
    cap_ref,
    blk_ref,
    rowb_ref,
    colb_ref,
    density_ref,
    vel_ref,
    edge_part,
    part_recv,
    edge_recv,
    wedge_send,
    wedge_recv,
    w_send,
    w_plane,
    w_block,
    rowb_high,
    rowb_low,
    colb_parts,
    rim_send,
    rim_recv,
    field_send,
    field_plane,
    field_block,
    padded,
    answer_send,
    answer_near,
    near_send,
    near,
    still_send,
    still_recv,
    still_all,
    tops_send,
    tops_recv,
    tops_all,
    inflow,
    last_send,
    last_recv,
    send_sem,
    recv_sem,
):
    K, Q, C, RD, NC, BL = sizes
    strips = K * Q
    HC = w_send.shape[2]
    cut = NC - HC
    depth = Q // 2
    strip = lax.axis_index("strip")
    cell = lax.axis_index("cells")
    plane = strip // Q
    place = strip % Q
    half = strip % 2
    first_cell, last_cell = cell == 0, cell == C - 1
    first_plane, last_plane = plane == 0, plane == K - 1

    def at(strip_id, cell_id):
        return (strip_id, cell_id)

    cell_peers = [at(strip, (cell + d) % C) for d in range(1, C)]
    above_strip, below_strip = (strip + strips - 1) % strips, (strip + 1) % strips
    offsets = [(dz, dy) for dz in range(depth) for dy in range(2) if (dz, dy) != (0, 0)]
    offsets.sort(key=lambda o: -(min(o[0], depth - o[0]) + 2 * o[1]))
    plane_peers = []
    for dz, dy in offsets:
        other = ((place // 2 + dz) % depth) * 2 + (place % 2 + dy) % 2
        plane_peers.append((at(plane * Q + other, cell), (half + dy) % 2))
    partner = at(strip + 1 - 2 * half, cell)
    shifts = [(dk, dy) for dk in range(K) for dy in range(2) if (dk, dy) != (0, 0)]
    shifts.sort(key=lambda o: -(min(o[0], K - o[0]) + 2 * o[1]))
    plane_cross = [
        at(((plane + dk) % K) * Q + place + dy * (1 - 2 * half), cell) for dk, dy in shifts
    ]
    slot = 2 * plane + half
    row_peers = [at(s, (cell + d) % C) for s in (above_strip, below_strip) for d in range(C)]

    barrier = pltpu.get_barrier_semaphore()
    greeted = cell_peers + [p for p, _ in plane_peers] + plane_cross + row_peers
    for peer in greeted:
        pl.semaphore_signal(barrier, 1, device_id=peer, device_id_type=pl.DeviceIdType.MESH)

    sent = []

    def send(group, source, target, peer):
        pltpu.make_async_remote_copy(
            src_ref=source,
            dst_ref=target,
            send_sem=send_sem.at[group],
            recv_sem=recv_sem.at[group],
            device_id=peer,
            device_id_type=pl.DeviceIdType.MESH,
        ).start()

    def arrived(group, span):
        sent.append((group, span))
        pltpu.make_async_copy(span, span, recv_sem.at[group]).wait()

    weights = cap_ref[...].astype(f32) * (1.0 - blk_ref[...])
    w_send[0] = weights[:, :HC]
    w_send[1] = weights[:, cut:]
    w_plane[place] = w_send[half]
    wedge_send[0] = weights[:1]
    wedge_send[1] = weights[RD - 1 :]
    for c in range(C):
        edge_part[0, c] = part_ref[c, :1]
        edge_part[1, c] = part_ref[c, RD - 1 :]
    pl.semaphore_wait(barrier, len(greeted))

    for d in range(C):
        other = (cell + d) % C
        send(1, edge_part.at[0, other], edge_recv.at[1, cell], at(above_strip, other))
        send(1, edge_part.at[1, other], edge_recv.at[0, cell], at(below_strip, other))
    send(2, wedge_send.at[0], wedge_recv.at[1], at(above_strip, cell))
    send(2, wedge_send.at[1], wedge_recv.at[0], at(below_strip, cell))
    for d in range(1, C):
        other = (cell + d) % C
        send(0, part_ref.at[other], part_recv.at[C - 1 - d], at(strip, other))
    for peer, other_half in plane_peers:
        send(3, w_send.at[other_half], w_plane.at[place], peer)

    for n in range(rowb_ref.shape[0]):
        high, low = exact_parts(rowb_ref[n])
        rowb_high[n] = high
        rowb_low[n] = low
    high, low = exact_parts(colb_ref[plane])
    colb_parts[0] = high
    colb_parts[1] = low

    end = lax.broadcasted_iota(jnp.int32, (RD, HC), 1)

    def along_inside(values):
        left = pltpu.roll(values, 1, 1)
        right = pltpu.roll(values, NC - 1, 1)
        spot = lax.broadcasted_iota(jnp.int32, values.shape, 1)
        left = jnp.where(spot == 0, jnp.where(first_cell, values, 0.0), left)
        right = jnp.where(spot == NC - 1, jnp.where(last_cell, values, 0.0), right)
        return 2.0 * values - left - right

    weights_two = jnp.concatenate([weights, weights], axis=0)
    spot = lax.broadcasted_iota(jnp.int32, (2 * RD, NC), 1)
    row = lax.broadcasted_iota(jnp.int32, (2 * RD, NC), 0)
    unit = jnp.where(spot == jnp.where(row < RD, 0, NC - 1), coupling, 0.0)
    pulse = row_product(unit, rowb_high, rowb_low)
    pulses = [pulse]
    for _ in range(SWEEPS - 1):
        back = weights_two * pulse + coupling * along_inside(pulse)
        pulse = pulse - row_product(back, rowb_high, rowb_low)
        pulses.append(pulse)

    arrived(1, edge_recv)
    arrived(2, wedge_recv)
    arrived(0, part_recv.at[0 : C - 1])
    density = part_ref[cell]
    for d in range(C - 1):
        density = density + part_recv[d]
    current = density / weights
    row_above = edge_recv[0, 0]
    row_below = edge_recv[1, 0]
    for c in range(1, C):
        row_above = row_above + edge_recv[0, c]
        row_below = row_below + edge_recv[1, c]
    row_above = row_above / wedge_recv[0]
    row_below = row_below / wedge_recv[1]
    row_above = jnp.where(strip == 0, current[:1], row_above)
    row_below = jnp.where(strip == strips - 1, current[RD - 1 :], row_below)

    def frames():
        base = pl.multiple_of(RD * 2 * (place // 2), 2 * RD)
        inner = padded[pl.ds(base + 8, 2 * RD), :]
        over = padded[pl.ds(base + 7, 1), :]
        under = padded[pl.ds(base + 8 + 2 * RD, 1), :]
        fill = jnp.zeros((6 - RD, HC), f32)
        upper = jnp.concatenate([over, inner[: RD + 1], fill], axis=0)
        lower = jnp.concatenate([inner[RD - 1 :], under, fill], axis=0)
        return jnp.where(half == 0, upper, lower), jnp.where(half == 0, lower, upper)

    small = lax.broadcasted_iota(jnp.int32, (RD, 128), 1)

    def clamp_rows(values):
        shape = values.shape
        spot = lax.broadcasted_iota(jnp.int32, shape, 0)
        up = pltpu.roll(values, 1, 0)
        down = pltpu.roll(values, shape[0] - 1, 0)
        up = jnp.where(spot == 0, jnp.where(first_plane, values, 0.0), up)
        down = jnp.where(spot == shape[0] - 1, jnp.where(last_plane, values, 0.0), down)
        return 2.0 * values - up - down

    for step in range(STEPS):
        up = jnp.concatenate([row_above, current[: RD - 1]], axis=0)
        down = jnp.concatenate([current[1:], row_below], axis=0)
        source = weights * current - coupling * (2.0 * current - up - down)
        iterate = current
        levels = [iterate]
        for _ in range(SWEEPS):
            left_over = source - (weights * iterate + coupling * along_inside(iterate))
            iterate = iterate + row_product(left_over, rowb_high, rowb_low)
            levels.append(iterate)
        for side, column in ((0, 0), (1, NC - 1)):
            message = jnp.zeros((RD, 128), f32)
            for j in range(SWEEPS + 1):
                message = jnp.where(small == j, levels[j][:, column : column + 1], message)
            for m in range(SWEEPS):
                mine = pulses[m][side * RD : (side + 1) * RD, column : column + 1]
                message = jnp.where(small == SWEEPS + 1 + m, mine, message)
            rim_send[step, side] = message
        group = 4 + 4 * step
        send(group, rim_send.at[step, 0], rim_recv.at[step, 1], at(strip, (cell + C - 1) % C))
        send(group, rim_send.at[step, 1], rim_recv.at[step, 0], at(strip, (cell + 1) % C))

        if step == 0:
            arrived(3, w_plane.at[0 : Q - 1])
            for i in range(Q):
                w_block[RD * i : RD * (i + 1), :] = w_plane[i]
            padded[0:8, :] = jnp.zeros((8, HC), f32)
            padded[BL + 8 :, :] = jnp.zeros((8, HC), f32)
            for side, column in ((0, 0), (1, BL - 1)):
                answer = coupling * jnp.broadcast_to(
                    colb_ref[plane][:, column : column + 1], (BL, HC)
                )
                for m in range(SWEEPS):
                    if m > 0:
                        back = w_block[...] * answer + coupling * clamp_rows(answer)
                        answer = answer - col_product(colb_parts, back)
                    padded[8 : BL + 8, :] = answer
                    own, other = frames()
                    answer_near[half, m, side] = own
                    answer_send[m, side] = other
                    still_send[m, side, 0:1, :] = answer[:1]
                    still_send[m, side, 1:2, :] = answer[BL - 1 :]
            still_recv[slot] = still_send[...]
            for peer in plane_cross:
                send(5, still_send, still_recv.at[slot], peer)
            send(9, answer_send, answer_near.at[half], partner)

        arrived(group, rim_recv.at[step])
        edges = []
        for side in range(2):
            own = [rim_send[step, side][:, i : i + 1] for i in range(2 * SWEEPS + 1)]
            far = [rim_recv[step, side][:, i : i + 1] for i in range(2 * SWEEPS + 1)]
            mine, theirs = [], []
            for j in range(SWEEPS + 1):
                a, b = own[j], far[j]
                for i in range(j):
                    a = a + own[SWEEPS + j - i] * theirs[i]
                    b = b + far[SWEEPS + j - i] * mine[i]
                mine.append(a)
                theirs.append(b)
            edges.append(theirs)
        left_in = [jnp.where(first_cell, 0.0, e) for e in edges[0]]
        right_in = [jnp.where(last_cell, 0.0, e) for e in edges[1]]
        for i in range(SWEEPS):
            iterate = iterate + (
                pulses[SWEEPS - 1 - i][:RD] * left_in[i] + pulses[SWEEPS - 1 - i][RD:] * right_in[i]
            )
        halo_left = jnp.where(first_cell, iterate[:, :1], left_in[SWEEPS])
        halo_right = jnp.where(last_cell, iterate[:, NC - 1 :], right_in[SWEEPS])
        field_send[step, 0] = jnp.where(end == HC - 1, halo_left, iterate[:, :HC])
        field_send[step, 1] = jnp.where(end == 0, halo_right, iterate[:, cut:])
        field_plane[step, place] = field_send[step, half]
        for peer, other_half in plane_peers:
            send(group + 2, field_send.at[step, other_half], field_plane.at[step, place], peer)
        arrived(group + 2, field_plane.at[step, 0 : Q - 1])
        for i in range(Q):
            field_block[RD * i : RD * (i + 1), :] = field_plane[step, i]

        start = field_block[...]
        beside = pltpu.roll(start, 1, 1) + pltpu.roll(start, HC - 1, 1)
        middle = w_block[...] * start - coupling * (2.0 * start - beside)
        iterate = start
        for j in range(SWEEPS + 1):
            if j > 0:
                left_over = middle - (w_block[...] * iterate + coupling * clamp_rows(iterate))
                iterate = iterate + col_product(colb_parts, left_over)
            tops_send[step, j, 0:1, :] = iterate[:1]
            tops_send[step, j, 1:2, :] = iterate[BL - 1 :]
        for peer in plane_cross:
            send(group + 3, tops_send.at[step], tops_recv.at[step, slot], peer)
        padded[8 : BL + 8, :] = iterate
        own, other = frames()
        near_send[step] = other
        near[step, half] = own
        send(13 + step, near_send.at[step], near.at[step, half], partner)
        tops_recv[step, slot] = tops_send[step]

        if step == 0:
            arrived(5, still_recv.at[0 : 2 * K - 1])
            arrived(9, answer_near.at[0])
            for k in range(K):
                for m in range(SWEEPS):
                    for side in range(2):
                        for h in range(2):
                            still_all[h, m, side, 2 * k : 2 * k + 2, :] = still_recv[
                                2 * k + h, m, side
                            ]
        arrived(group + 3, tops_recv.at[step, 0 : 2 * K - 1])
        for k in range(K):
            for j in range(SWEEPS + 1):
                for h in range(2):
                    tops_all[h, j, 2 * k : 2 * k + 2, :] = tops_recv[step, 2 * k + h, j]
        arrived(13 + step, near.at[step, 0])
        spot = lax.broadcasted_iota(jnp.int32, (2 * K, HC), 0)
        even = spot % 2 == 0
        mine = pl.ds(2 * plane, 1)
        halves = []
        for h in range(2):
            from_above, from_below = [], []
            for j in range(SWEEPS + 1):
                value = tops_all[h, j]
                for i in range(j):
                    value = value + still_all[h, j - i - 1, 0] * from_above[i]
                    value = value + still_all[h, j - i - 1, 1] * from_below[i]
                over = jnp.where(even, pltpu.roll(value, 1, 0), pltpu.roll(value, 2, 0))
                under = jnp.where(
                    even, pltpu.roll(value, 2 * K - 2, 0), pltpu.roll(value, 2 * K - 1, 0)
                )
                from_above.append(jnp.where(spot < 2, 0.0, over))
                from_below.append(jnp.where(spot >= 2 * K - 2, 0.0, under))
                inflow[h, j, 0] = from_above[j]
                inflow[h, j, 1] = from_below[j]
            nearby = near[step, h]
            for i in range(SWEEPS):
                m = SWEEPS - 1 - i
                nearby = nearby + (
                    answer_near[h, m, 0] * inflow[h, i, 0, mine, :]
                    + answer_near[h, m, 1] * inflow[h, i, 1, mine, :]
                )
            above, below = nearby[:1], nearby[1 + RD : 2 + RD]
            above = jnp.where(place == 0, inflow[h, SWEEPS, 0, mine, :], above)
            below = jnp.where(place == Q - 1, inflow[h, SWEEPS, 1, mine, :], below)
            halves.append((above, nearby[1 : 1 + RD], below))

        def joined(first, second):
            over = HC - cut
            lanes = lax.broadcasted_iota(jnp.int32, (first.shape[0], over), 1)
            both = jnp.where(lanes < over // 2, first[:, cut:], second[:, :over])
            return jnp.concatenate([first[:, :cut], both, second[:, over:]], axis=1)

        row_above, current, row_below = (joined(a, b) for a, b in zip(*halves))
        row_above = jnp.where(strip == 0, current[:1], row_above)
        row_below = jnp.where(strip == strips - 1, current[RD - 1 :], row_below)

    density_ref[...] = current
    last_send[0:1, :] = row_above
    last_send[1 : 1 + RD, :] = current
    last_send[1 + RD : 2 + RD, :] = row_below
    last_send[2 + RD : 8, :] = jnp.zeros((6 - RD, NC), f32)
    last_recv[cell] = last_send[...]
    for peer in cell_peers:
        send(12, last_send, last_recv.at[cell], peer)
    arrived(12, last_recv.at[0 : C - 1])
    field = jnp.concatenate([last_recv[c] for c in range(C)], axis=1)
    centre = field[1 : 1 + RD]
    spot = lax.broadcasted_iota(jnp.int32, (RD, C * NC), 1)
    left = jnp.where(spot == 0, centre, pltpu.roll(centre, 1, 1))
    right = jnp.where(spot == C * NC - 1, centre, pltpu.roll(centre, C * NC - 1, 1))
    scale = jnp.maximum(centre, floor_level)
    vel_ref[0] = -(0.5 * (field[2 : 2 + RD] - field[:RD])) / scale
    vel_ref[1] = -(0.5 * (right - left)) / scale
    for group, span in sent:
        pltpu.make_async_copy(span, span, send_sem.at[group]).wait()


def diffuse(part, capacity, blockage, row_blocks, col_blocks):
    strips = lax.axis_size("strip")
    C = lax.axis_size("cells")
    RD, NC = capacity.shape
    NB = row_blocks.shape[0]
    K, BL = col_blocks.shape[:2]
    Q = strips // K
    HC = 128 * ((NB + 1) // 2)
    vmem = pl.BlockSpec(memory_space=pltpu.VMEM)
    shapes = [
        ((2, C, 1, NC), f32),
        ((C, RD, NC), f32),
        ((2, C, 1, NC), f32),
        ((2, 1, NC), f32),
        ((2, 1, NC), f32),
        ((2, RD, HC), f32),
        ((Q, RD, HC), f32),
        ((BL, HC), f32),
        ((NB, 128, 128), bf16),
        ((NB, 128, 128), bf16),
        ((2, BL, BL), bf16),
        ((STEPS, 2, RD, 128), f32),
        ((STEPS, 2, RD, 128), f32),
        ((STEPS, 2, RD, HC), f32),
        ((STEPS, Q, RD, HC), f32),
        ((BL, HC), f32),
        ((BL + 16, HC), f32),
        ((SWEEPS, 2, 8, HC), f32),
        ((2, SWEEPS, 2, 8, HC), f32),
        ((STEPS, 8, HC), f32),
        ((STEPS, 2, 8, HC), f32),
        ((SWEEPS, 2, 2, HC), f32),
        ((2 * K, SWEEPS, 2, 2, HC), f32),
        ((2, SWEEPS, 2, 2 * K, HC), f32),
        ((STEPS, SWEEPS + 1, 2, HC), f32),
        ((STEPS, 2 * K, SWEEPS + 1, 2, HC), f32),
        ((2, SWEEPS + 1, 2 * K, HC), f32),
        ((2, SWEEPS + 1, 2, 2 * K, HC), f32),
        ((8, NC), f32),
        ((C, 8, NC), f32),
    ]
    return pl.pallas_call(
        functools.partial(adi_kernel, (K, Q, C, RD, NC, BL)),
        out_shape=(
            jax.ShapeDtypeStruct((RD, NC), f32),
            jax.ShapeDtypeStruct((2, RD, C * NC), f32),
        ),
        in_specs=[vmem] * 5,
        out_specs=(vmem, vmem),
        scratch_shapes=[pltpu.VMEM(shape, dtype) for shape, dtype in shapes]
        + [pltpu.SemaphoreType.DMA((15,)), pltpu.SemaphoreType.DMA((15,))],
        compiler_params=pltpu.CompilerParams(
            collective_id=0, has_side_effects=True, vmem_limit_bytes=48 << 20
        ),
        name="adi",
    )(part, capacity, blockage, row_blocks, col_blocks)


def pin_tables(block_rows, block_cols, row_near, row_far, col_near, col_far, rows_dev, hi_count):
    block_size = block_rows.shape[0]
    zero_value = jnp.zeros((), jnp.bfloat16)
    row_index = lax.broadcasted_iota(jnp.int32, (block_size, rows_dev), 1)
    row_table = jnp.where(
        row_index == block_rows[:, None], row_near[:, None], zero_value
    ) + jnp.where(row_index == block_rows[:, None] + 1, row_far[:, None], zero_value)
    high_index = lax.broadcasted_iota(jnp.int32, (block_size, 1, hi_count), 2)
    low_index = lax.broadcasted_iota(jnp.int32, (block_size, 128), 1)
    bin_tables = []
    lane_tables = []
    for offset, factor in ((0, col_near), (1, col_far)):
        column = block_cols + offset
        high_part = column // 128
        low_part = column - high_part * 128
        chosen = (high_index == high_part[:, None, None]).astype(jnp.bfloat16)
        bin_tables.append((row_table[:, :, None] * chosen).reshape(block_size, rows_dev * hi_count))
        lane_tables.append(jnp.where(low_index == low_part[:, None], factor[:, None], zero_value))
    return (jnp.concatenate(bin_tables, 0), jnp.concatenate(lane_tables, 0))


def pin_factors(pin_rows, pin_cols, row_near, row_far, col_near, col_far):
    block_size = min(2048, pin_rows.shape[0])
    return (
        block_size,
        tuple(
            (
                item.reshape(-1, block_size)
                for item in (pin_rows, pin_cols, row_near, row_far, col_near, col_far)
            )
        ),
    )


def splat(pin_rows, pin_cols, pin_fracs, pin_weights, rows_dev, hi_count):
    near_y = 1.0 - pin_fracs[0]
    near_x = 1.0 - pin_fracs[1]
    block_size, pieces = pin_factors(
        pin_rows,
        pin_cols,
        (pin_weights * near_y).astype(jnp.bfloat16),
        (pin_weights * pin_fracs[0]).astype(jnp.bfloat16),
        near_x.astype(jnp.bfloat16),
        pin_fracs[1].astype(jnp.bfloat16),
    )

    def add_block(total, block):
        bins, lane_table = pin_tables(
            block[0], block[1], block[2], block[3], block[4], block[5], rows_dev, hi_count
        )
        part_sum = lax.dot_general(
            bins, lane_table, (((0,), (0,)), ((), ())), preferred_element_type=jnp.float32
        )
        return (total + part_sum, None)

    total, unused = lax.scan(add_block, jnp.zeros((rows_dev * hi_count, 128), jnp.float32), pieces)
    return total.reshape(rows_dev, hi_count * 128)


def interpolate(pin_rows, pin_cols, pin_fracs, velocity_y, velocity_x, rows_dev, hi_count):
    stacked = jnp.concatenate(
        [
            velocity_y.reshape(rows_dev * hi_count, 128),
            velocity_x.reshape(rows_dev * hi_count, 128),
        ],
        1,
    )
    npins = pin_rows.shape[0]
    block_size, pieces = pin_factors(
        pin_rows,
        pin_cols,
        (1.0 - pin_fracs[0]).astype(jnp.bfloat16),
        pin_fracs[0].astype(jnp.bfloat16),
        (1.0 - pin_fracs[1]).astype(jnp.bfloat16),
        pin_fracs[1].astype(jnp.bfloat16),
    )

    def one_block(carry, block):
        bins, lane_table = pin_tables(
            block[0], block[1], block[2], block[3], block[4], block[5], rows_dev, hi_count
        )
        sampled = jnp.dot(bins, stacked, preferred_element_type=jnp.float32)
        lane_values = lane_table.astype(jnp.float32)
        both_y = jnp.sum(sampled[:, :128] * lane_values, axis=1)
        both_x = jnp.sum(sampled[:, 128:] * lane_values, axis=1)
        result = jnp.stack(
            [both_y[:block_size] + both_y[block_size:], both_x[:block_size] + both_x[block_size:]]
        )
        return (carry, result)

    unused, outputs = lax.scan(one_block, jnp.zeros((), jnp.float32), pieces)
    return jnp.transpose(outputs, (1, 0, 2)).reshape(2, npins)


def local(pin_rows, pin_cols, pin_fracs, pin_weights, capacity, blockage, row_blocks, col_blocks):
    rows_dev, cols_dev = capacity.shape
    cells = lax.axis_size("cells")
    hi_count = cols_dev * cells // 128
    part = splat(pin_rows, pin_cols, pin_fracs, pin_weights, rows_dev, hi_count)
    part = jnp.transpose(part.reshape(rows_dev, cells, cols_dev), (1, 0, 2))
    current, velocity = diffuse(part, capacity, blockage, row_blocks, col_blocks)
    velocity = velocity.astype(bf16)
    pin_velocity = interpolate(
        pin_rows, pin_cols, pin_fracs, velocity[0], velocity[1], rows_dev, hi_count
    )
    return (current, pin_velocity)


def solution(mesh):
    placed = (
        P(("strip", "cells")),
        P(("strip", "cells")),
        P(None, ("strip", "cells")),
        P(("strip", "cells")),
        P("strip", "cells"),
        P("strip", "cells"),
        P("cells", None, None),
        P(),
    )
    return jax.shard_map(
        local,
        mesh=mesh,
        in_specs=placed,
        out_specs=(P("strip", "cells"), P(None, ("strip", "cells"))),
        check_vma=False,
    )
```

time: 362 us -> 86.3 us (0.24)
  waiting for transfers between devices: 141 us -> 0 us
  starting transfers between devices: 125 us -> 0 us
  Pallas kernels: 0 us -> 71.6 us
  blocking collectives: 55.3 us -> 0 us
  local copies, waits for them, and re-layouts: 20.3 us -> 4.19 us
  matrix products: 9.52 us -> 2.17 us
    all_to_all x7 -> x0, waiting for transfers between devices: 120 us -> none  [the longest x2 42.3 us: local(): lax.all_to_all(middle.T, 'strip', split_axis=0, concat_axis=1, tiled=True)]
    all_to_all x7 -> x0, starting transfers between devices: 77.5 us -> none  [the longest x2 25.3 us: local(): lax.all_to_all(current.T, 'strip', split_axis=0, concat_axis=1, tiled=True)]
    pallas_call x0 -> x1, Pallas kernels: none -> 71.6 us  [diffuse(): pl.pallas_call(functools.partial(adi_kernel, (K, Q, C, RD, NC, BL)), out_...]
    ppermute x20 -> x0, starting transfers between devices: 47.1 us -> none  [the longest x10 23.9 us: padded_2(): lax.ppermute(lax.slice_in_dim(block, 0, width, axis=dim), axis, backward)]
    all_to_all x1 -> x0, blocking collectives: 28.3 us -> none  [local(): lax.all_to_all(current_col, 'strip', split_axis=1, concat_axis=0, tiled=T...]
    ppermute x20 -> x0, waiting for transfers between devices: 20.5 us -> none  [the longest x10 20.5 us: padded_2(): lax.ppermute(lax.slice_in_dim(block, 0, width, axis=dim), axis, backward)]
    psum x1 -> x0, blocking collectives: 16.6 us -> none  [local(): whole = lax.psum(partial_value, 'cells')]
    all_gather x1 -> x0, blocking collectives: 10.5 us -> none  [local(): strip_field = lax.all_gather(extended, 'cells', axis=1, tiled=True)]
  transfers between devices with their start and end apart: 27 -> 0, of which waited for: 14 -> 0; matrix products, arithmetic and copies ran while one was open for 3% -> 0% of each run, Pallas kernels for 0% -> 0%
where the time goes in v1:
time: 86.3 us; the launch traced here: 85.9 us
  Pallas kernels  71.6 us (83%)
  other arithmetic  6.64 us (8%)
  local copies, waits for them, and re-layouts  4.19 us (5%)
  matrix products  2.17 us (3%)
    pallas_call x1, Pallas kernels, diffuse(): pl.pallas_call(functools.partial(adi_kernel, (K, Q, C, RD, NC, BL)), out_...  71.6 us
    select_n x8, other arithmetic, pin_tables(): jnp.where(low_index == low_part[:, None], factor[:, None], zero_value)  3.24 us

profile of v1, /device:TPU:1, one launch (start us, length us, event | category | flops | bytes accessed | tf_op | source)
XLA Modules:
  0.0 85.9 jit_solution(17177332502689194511)
XLA Ops:
  0.6 1.0 %convert_reduce_fusion = (bf16[4096]{0:T(1024)(128)(2,1)S(1)}, bf16[4096]{0:T(1024)(128)(2,1)S(1)}, bf16[4096]{0:T(1024)(128)(2,1)S(1)}, bf16[4096]{0:T(1024)(128)(2,1)S(1)}) fusion(f32[2,4096]{1,0:T(2,128)} %param.14), kind=kLoop, calls=%fused_computation.100 | loop fusion | flops 24576 | bytes 65536 | tf_op jit(solution)/shard_map/convert_element_type | solution.py:532
  1.7 0.8 slice.60
  2.4 0.7 multiply_convert_fusion
  3.2 0.7 reshape.643
  3.9 0.7 reshape.646
  4.7 4.6 %while.28 = (s32[]{:T(128)}, f32[80,128]{1,0:T(8,128)S(1)}, s32[2,2048]{1,0:T(2,128)S(1)}, bf16[2,2048]{1,0:T(2,128)(2,1)S(1)}, bf16[2,2048]{1,0:T(2,128)(2,1)S(...) while((s32[]{:T(128)}, f32[80,128]{1,0:T(8,128)S(1)}, ...), condition=%wide.region_1.2_spmd.clone, body=%wide.region_0.1_spmd.clone.sunk | while | flops 88993792 | bytes 5349499 | solution.py:515
  4.8 0.1 dynamic-slice_reduce_fusion.15
  5.0 0.1 mul.207
  5.1 0.1 mul.208
  5.2 0.7 fusion.68
  6.0 0.7 fusion.69
  6.7 0.3 convolution_add_fusion.2
  7.3 0.1 mul.207
  7.4 0.1 mul.208
  7.6 0.7 fusion.68
  8.3 0.7 fusion.69
  9.0 0.3 convolution_add_fusion.2
  9.4 71.6 %adi.1 = (f32[4,640]{1,0:T(4,128)S(1)}, f32[2,4,2560]{2,1,0:T(4,128)S(1)}) custom-call(f32[4,4,640]{2,1,0:T(4,128)S(1)} %bitcast.42, s32[4,640]{1,0:T(4,128)S(1)} %copy-done.2, f32[4,640]{1,0:T(4,128)S(1)} %copy-done.3, f32[5,128,128]{2,1,0:T(8,128)S(1)} %copy-done, f32[4,128,128]{2,1,0:T(8,128)S(1)} %copy-done.1), custom_call_target="tpu_custom_call" | custom-call | tf_op jit(solution)/shard_map/adi/pallas_call | solution.py:443
  81.2 4.1 %while.27 = (s32[]{:T(128)}, f32[2,2,2048]{2,1,0:T(2,128)S(1)}, s32[2,2048]{1,0:T(2,128)S(1)}, bf16[2,2048]{1,0:T(2,128)(2,1)S(1)}, bf16[2,2048]{1,0:T(2,128)(2,...) while((s32[]{:T(128)}, f32[2,2,2048]{2,1,0:T(2,128)S(1)}, ...), condition=%wide.region_5.6_spmd, body=%wide.region_2.5_spmd.sunk | while | flops 174956544 | bytes 13811829 | solution.py:550
  81.5 0.1 mul.202
  81.6 0.1 mul.203
  81.7 0.7 fusion.61
  82.5 0.1 fusion.62
  82.6 0.1 fusion.63
  82.7 0.5 fusion.64
  83.5 0.1 mul.202
  83.6 0.1 mul.203
  83.7 0.7 fusion.61
  84.5 0.1 fusion.62
  84.6 0.1 fusion.63
  84.7 0.5 fusion.64
  85.3 0.6 copy.31
  (66 shorter events, 1.4 us)
Async XLA Ops:
  4.7 4.7 %copy-start = (f32[5,128,128]{2,1,0:T(8,128)S(1)}, f32[5,128,128]{2,1,0:T(8,128)}, u32[]{:S(2)}) copy-start(f32[5,128,128]{2,1,0:T(8,128)} %rowb_ref.1) | copy-start | bytes 983044
  4.7 4.7 %copy-start.1 = (f32[4,128,128]{2,1,0:T(8,128)S(1)}, f32[4,128,128]{2,1,0:T(8,128)}, u32[]{:S(2)}) copy-start(f32[4,128,128]{2,1,0:T(8,128)} %colb_ref.1) | copy-start | bytes 786436
  4.7 4.7 %copy-start.2 = (s32[4,640]{1,0:T(4,128)S(1)}, s32[4,640]{1,0:T(4,128)}, u32[]{:S(2)}) copy-start(s32[4,640]{1,0:T(4,128)} %cap_ref.1) | copy-start | bytes 30724
  4.7 4.7 %copy-start.3 = (f32[4,640]{1,0:T(4,128)S(1)}, f32[4,640]{1,0:T(4,128)}, u32[]{:S(2)}) copy-start(f32[4,640]{1,0:T(4,128)} %blk_ref.1) | copy-start | bytes 30724
  85.3 0.6 copy-start.4

commit v2 on v1

--- a/solution.py
+++ b/solution.py
@@ -20,33 +20,57 @@
     return high, (values - high.astype(f32)).astype(bf16)
 
 
-def row_product(values, high_ref, low_ref):
+def row_product(values, blocks_ref):
     pieces = []
-    for n in range(high_ref.shape[0]):
+    for n in range(blocks_ref.shape[0]):
         high, low = exact_parts(values[:, 128 * n : 128 * (n + 1)])
-        dims = (((1,), (1,)), ((), ()))
-        dot = functools.partial(lax.dot_general, dimension_numbers=dims, preferred_element_type=f32)
         pieces.append(
-            dot(high, high_ref[n]) + (dot(low, high_ref[n]) + dot(high, low_ref[n]))
+            lax.dot_general(
+                jnp.concatenate([high, low, high], axis=1),
+                blocks_ref[n],
+                (((1,), (1,)), ((), ())),
+                preferred_element_type=f32,
+            )
         )
     return jnp.concatenate(pieces, axis=1)
 
 
-def col_product(matrix, values):
+def col_product(matrix_ref, values):
     high, low = exact_parts(values)
-    dot = functools.partial(jnp.dot, preferred_element_type=f32)
-    return dot(matrix[0], high) + (dot(matrix[0], low) + dot(matrix[1], high))
+    parts = jnp.concatenate([high, low, high], axis=0)
+    return jnp.dot(matrix_ref[...], parts, preferred_element_type=f32)
+
+
+def table(index, first, second, count):
+    spot = lax.broadcasted_iota(jnp.int32, (count, index.shape[1]), 0)
+    return jnp.where(spot == index, first, jnp.where(spot == index + 1, second, 0.0))
 
 
 def adi_kernel(
     sizes,
-    part_ref,
+    rows_hbm,
+    cols_hbm,
+    fracs_hbm,
+    pinw_hbm,
+    cap_hbm,
+    blk_hbm,
+    rowb_hbm,
+    colb_hbm,
+    density_ref,
+    pinv_ref,
+    rows_ref,
+    cols_ref,
+    pinw_ref,
+    fracs_ref,
     cap_ref,
     blk_ref,
     rowb_ref,
     colb_ref,
-    density_ref,
-    vel_ref,
+    bin_sums,
+    part_ref,
+    look,
+    spread,
+    vel_bins,
     edge_part,
     part_recv,
     edge_recv,
@@ -55,8 +79,7 @@
     w_send,
     w_plane,
     w_block,
-    rowb_high,
-    rowb_low,
+    rowb_parts,
     colb_parts,
     rim_send,
     rim_recv,
@@ -79,17 +102,19 @@
     last_recv,
     send_sem,
     recv_sem,
+    load_sem,
 ):
     K, Q, C, RD, NC, BL = sizes
     strips = K * Q
     HC = w_send.shape[2]
     cut = NC - HC
-    depth = Q // 2
     strip = lax.axis_index("strip")
     cell = lax.axis_index("cells")
     plane = strip // Q
     place = strip % Q
-    half = strip % 2
+    depth = Q // 2
+    half = (place // 2) % 2
+    strip_side = place % 2
     first_cell, last_cell = cell == 0, cell == C - 1
     first_plane, last_plane = plane == 0, plane == K - 1
 
@@ -103,12 +128,12 @@
     plane_peers = []
     for dz, dy in offsets:
         other = ((place // 2 + dz) % depth) * 2 + (place % 2 + dy) % 2
-        plane_peers.append((at(plane * Q + other, cell), (half + dy) % 2))
-    partner = at(strip + 1 - 2 * half, cell)
-    shifts = [(dk, dy) for dk in range(K) for dy in range(2) if (dk, dy) != (0, 0)]
-    shifts.sort(key=lambda o: -(min(o[0], K - o[0]) + 2 * o[1]))
+        plane_peers.append((at(plane * Q + other, cell), (half + dz) % 2))
+    partner = at(strip + 2 - 4 * half, cell)
+    shifts = [(dk, dz) for dk in range(K) for dz in range(2) if (dk, dz) != (0, 0)]
+    shifts.sort(key=lambda o: -(min(o[0], K - o[0]) + o[1]))
     plane_cross = [
-        at(((plane + dk) % K) * Q + place + dy * (1 - 2 * half), cell) for dk, dy in shifts
+        at(((plane + dk) % K) * Q + place + dz * (2 - 4 * half), cell) for dk, dz in shifts
     ]
     slot = 2 * plane + half
     row_peers = [at(s, (cell + d) % C) for s in (above_strip, below_strip) for d in range(C)]
@@ -133,6 +158,60 @@
     def arrived(group, span):
         sent.append((group, span))
         pltpu.make_async_copy(span, span, recv_sem.at[group]).wait()
+
+    loads = [
+        pltpu.make_async_copy(source, target, load_sem.at[i])
+        for i, (source, target) in enumerate(
+            (
+                (rows_hbm, rows_ref),
+                (cols_hbm, cols_ref),
+                (pinw_hbm, pinw_ref),
+                (fracs_hbm, fracs_ref),
+                (cap_hbm, cap_ref),
+                (blk_hbm, blk_ref),
+                (rowb_hbm, rowb_ref),
+                (colb_hbm.at[plane], colb_ref),
+            )
+        )
+    ]
+    for load in loads:
+        load.start()
+    for load in loads:
+        load.wait()
+
+    chunks = rows_ref.shape[0]
+    bins = bin_sums.shape[0]
+
+    def pins_of(i):
+        span = pl.ds(pl.multiple_of(128 * i, 128), 128)
+        down, across = fracs_ref[0:1, span], fracs_ref[1:2, span]
+        column = cols_ref[pl.ds(i, 1), :]
+        tile = lax.shift_right_logical(column, 7)
+        return down, across, tile * RD + rows_ref[pl.ds(i, 1), :], column - tile * 128
+
+    def rounded(values):
+        return values.astype(bf16).astype(f32)
+
+    def add_pins(i, total):
+        down, across, index, lane = pins_of(i)
+        heavy = pinw_ref[pl.ds(i, 1), :]
+        where_down = table(index, rounded(heavy * (1.0 - down)), rounded(heavy * down), bins)
+        where_across = table(lane, rounded(1.0 - across), rounded(across), 136)
+        return total + lax.dot_general(
+            where_down.astype(bf16),
+            where_across.astype(bf16),
+            (((1,), (1,)), ((), ())),
+            preferred_element_type=f32,
+        )
+
+    total = lax.fori_loop(0, chunks, add_pins, jnp.zeros((bins, 136), f32), unroll=4)
+    spot = lax.broadcasted_iota(jnp.int32, (bins, 128), 1)
+    past = jnp.where(spot == 0, total[:, 128:129], 0.0)
+    bin_sums[...] = total[:, :128] + pltpu.roll(past, RD, 0)
+    for c in range(C):
+        for n in range(NC // 128):
+            tile = c * (NC // 128) + n
+            part_ref[c, :, 128 * n : 128 * (n + 1)] = bin_sums[RD * tile : RD * (tile + 1), :]
 
     weights = cap_ref[...].astype(f32) * (1.0 - blk_ref[...])
     w_send[0] = weights[:, :HC]
@@ -159,11 +238,9 @@
 
     for n in range(rowb_ref.shape[0]):
         high, low = exact_parts(rowb_ref[n])
-        rowb_high[n] = high
-        rowb_low[n] = low
-    high, low = exact_parts(colb_ref[plane])
-    colb_parts[0] = high
-    colb_parts[1] = low
+        rowb_parts[n] = jnp.concatenate([high, high, low], axis=1)
+    high, low = exact_parts(colb_ref[...])
+    colb_parts[...] = jnp.concatenate([high, high, low], axis=1)
 
     end = lax.broadcasted_iota(jnp.int32, (RD, HC), 1)
 
@@ -179,11 +256,11 @@
     spot = lax.broadcasted_iota(jnp.int32, (2 * RD, NC), 1)
     row = lax.broadcasted_iota(jnp.int32, (2 * RD, NC), 0)
     unit = jnp.where(spot == jnp.where(row < RD, 0, NC - 1), coupling, 0.0)
-    pulse = row_product(unit, rowb_high, rowb_low)
+    pulse = row_product(unit, rowb_parts)
     pulses = [pulse]
     for _ in range(SWEEPS - 1):
         back = weights_two * pulse + coupling * along_inside(pulse)
-        pulse = pulse - row_product(back, rowb_high, rowb_low)
+        pulse = pulse - row_product(back, rowb_parts)
         pulses.append(pulse)
 
     arrived(1, edge_recv)
@@ -203,15 +280,18 @@
     row_above = jnp.where(strip == 0, current[:1], row_above)
     row_below = jnp.where(strip == strips - 1, current[RD - 1 :], row_below)
 
-    def frames():
-        base = pl.multiple_of(RD * 2 * (place // 2), 2 * RD)
+    def frame(pair):
+        base = pl.multiple_of(RD * 2 * pair, 2 * RD)
         inner = padded[pl.ds(base + 8, 2 * RD), :]
         over = padded[pl.ds(base + 7, 1), :]
         under = padded[pl.ds(base + 8 + 2 * RD, 1), :]
         fill = jnp.zeros((6 - RD, HC), f32)
         upper = jnp.concatenate([over, inner[: RD + 1], fill], axis=0)
         lower = jnp.concatenate([inner[RD - 1 :], under, fill], axis=0)
-        return jnp.where(half == 0, upper, lower), jnp.where(half == 0, lower, upper)
+        return jnp.where(strip_side == 0, upper, lower)
+
+    def frames():
+        return frame(place // 2), frame(place // 2 + 1 - 2 * half)
 
     small = lax.broadcasted_iota(jnp.int32, (RD, 128), 1)
 
@@ -232,7 +312,7 @@
         levels = [iterate]
         for _ in range(SWEEPS):
             left_over = source - (weights * iterate + coupling * along_inside(iterate))
-            iterate = iterate + row_product(left_over, rowb_high, rowb_low)
+            iterate = iterate + row_product(left_over, rowb_parts)
             levels.append(iterate)
         for side, column in ((0, 0), (1, NC - 1)):
             message = jnp.zeros((RD, 128), f32)
@@ -245,31 +325,6 @@
         group = 4 + 4 * step
         send(group, rim_send.at[step, 0], rim_recv.at[step, 1], at(strip, (cell + C - 1) % C))
         send(group, rim_send.at[step, 1], rim_recv.at[step, 0], at(strip, (cell + 1) % C))
-
-        if step == 0:
-            arrived(3, w_plane.at[0 : Q - 1])
-            for i in range(Q):
-                w_block[RD * i : RD * (i + 1), :] = w_plane[i]
-            padded[0:8, :] = jnp.zeros((8, HC), f32)
-            padded[BL + 8 :, :] = jnp.zeros((8, HC), f32)
-            for side, column in ((0, 0), (1, BL - 1)):
-                answer = coupling * jnp.broadcast_to(
-                    colb_ref[plane][:, column : column + 1], (BL, HC)
-                )
-                for m in range(SWEEPS):
-                    if m > 0:
-                        back = w_block[...] * answer + coupling * clamp_rows(answer)
-                        answer = answer - col_product(colb_parts, back)
-                    padded[8 : BL + 8, :] = answer
-                    own, other = frames()
-                    answer_near[half, m, side] = own
-                    answer_send[m, side] = other
-                    still_send[m, side, 0:1, :] = answer[:1]
-                    still_send[m, side, 1:2, :] = answer[BL - 1 :]
-            still_recv[slot] = still_send[...]
-            for peer in plane_cross:
-                send(5, still_send, still_recv.at[slot], peer)
-            send(9, answer_send, answer_near.at[half], partner)
 
         arrived(group, rim_recv.at[step])
         edges = []
@@ -298,6 +353,40 @@
         field_plane[step, place] = field_send[step, half]
         for peer, other_half in plane_peers:
             send(group + 2, field_send.at[step, other_half], field_plane.at[step, place], peer)
+        if step == 0:
+            arrived(3, w_plane.at[0 : Q - 1])
+            for i in range(Q):
+                w_block[RD * i : RD * (i + 1), :] = w_plane[i]
+            padded[0:8, :] = jnp.zeros((8, HC), f32)
+            padded[BL + 8 :, :] = jnp.zeros((8, HC), f32)
+            for side, column in ((0, 0), (1, BL - 1)):
+                answer = coupling * jnp.broadcast_to(
+                    colb_ref[:, column : column + 1], (BL, HC)
+                )
+                for m in range(SWEEPS):
+                    if m > 0:
+                        back = w_block[...] * answer + coupling * clamp_rows(answer)
+                        answer = answer - col_product(colb_parts, back)
+                    padded[8 : BL + 8, :] = answer
+                    own, other = frames()
+                    answer_near[half, m, side] = own
+                    answer_send[m, side] = other
+                    still_send[m, side, 0:1, :] = answer[:1]
+                    still_send[m, side, 1:2, :] = answer[BL - 1 :]
+            still_recv[slot] = still_send[...]
+            for peer in plane_cross:
+                send(5, still_send, still_recv.at[slot], peer)
+            send(9, answer_send, answer_near.at[half], partner)
+        else:
+
+            def prepare(i, carry):
+                down, across, index, lane = pins_of(i)
+                look[i] = table(index, rounded(1.0 - down), rounded(down), 128).astype(bf16)
+                spread[i] = table(lane, rounded(1.0 - across), rounded(across), 136)
+                return carry
+
+            lax.fori_loop(0, chunks, prepare, 0, unroll=2)
+
         arrived(group + 2, field_plane.at[step, 0 : Q - 1])
         for i in range(Q):
             field_block[RD * i : RD * (i + 1), :] = field_plane[step, i]
@@ -393,13 +482,35 @@
     left = jnp.where(spot == 0, centre, pltpu.roll(centre, 1, 1))
     right = jnp.where(spot == C * NC - 1, centre, pltpu.roll(centre, C * NC - 1, 1))
     scale = jnp.maximum(centre, floor_level)
-    vel_ref[0] = -(0.5 * (field[2 : 2 + RD] - field[:RD])) / scale
-    vel_ref[1] = -(0.5 * (right - left)) / scale
+    velocity_y = -(0.5 * (field[2 : 2 + RD] - field[:RD])) / scale
+    velocity_x = -(0.5 * (right - left)) / scale
+    tables = []
+    for i, velocity in enumerate((velocity_y, velocity_x)):
+        vel_bins[i, bins:, :] = jnp.zeros((128 - bins, 128), f32)
+        for n in range(bins // RD):
+            vel_bins[i, RD * n : RD * (n + 1), :] = velocity[:, 128 * n : 128 * (n + 1)]
+        turned = jnp.transpose(vel_bins[i])
+        past = jnp.broadcast_to(pltpu.roll(turned[:8], 128 - RD, 1)[:1], (8, 128))
+        tables += [turned.astype(bf16), past.astype(bf16)]
+    tables = jnp.concatenate(tables, axis=0)
+
+    def sample(i, carry):
+        sampled = jnp.dot(tables, look[i], preferred_element_type=f32)
+        across = spread[i]
+        out_y = jnp.sum(sampled[:136] * across, axis=0, keepdims=True)
+        out_x = jnp.sum(sampled[136:] * across, axis=0, keepdims=True)
+        span = pl.ds(pl.multiple_of(128 * i, 128), 128)
+        pinv_ref[:, span] = jnp.concatenate([out_y, out_x], axis=0)
+        return carry
+
+    lax.fori_loop(0, chunks, sample, 0, unroll=4)
     for group, span in sent:
         pltpu.make_async_copy(span, span, send_sem.at[group]).wait()
 
 
-def diffuse(part, capacity, blockage, row_blocks, col_blocks):
+def diffuse(pin_rows, pin_cols, pin_fracs, pin_weights, capacity, blockage, row_blocks, col_blocks):
+    pins = pin_rows.shape[0]
+    chunks = pins // 128
     strips = lax.axis_size("strip")
     C = lax.axis_size("cells")
     RD, NC = capacity.shape
@@ -408,7 +519,21 @@
     Q = strips // K
     HC = 128 * ((NB + 1) // 2)
     vmem = pl.BlockSpec(memory_space=pltpu.VMEM)
+    bins = RD * C * NC // 128
     shapes = [
+        ((chunks, 128), jnp.int32),
+        ((chunks, 128), jnp.int32),
+        ((chunks, 128), f32),
+        ((2, pins), f32),
+        ((RD, NC), jnp.int32),
+        ((RD, NC), f32),
+        ((NB, 128, 128), f32),
+        ((BL, BL), f32),
+        ((bins, 128), f32),
+        ((C, RD, NC), f32),
+        ((chunks, 128, 128), bf16),
+        ((chunks, 136, 128), f32),
+        ((2, 128, 128), f32),
         ((2, C, 1, NC), f32),
         ((C, RD, NC), f32),
         ((2, C, 1, NC), f32),
@@ -417,9 +542,8 @@
         ((2, RD, HC), f32),
         ((Q, RD, HC), f32),
         ((BL, HC), f32),
-        ((NB, 128, 128), bf16),
-        ((NB, 128, 128), bf16),
-        ((2, BL, BL), bf16),
+        ((NB, 128, 384), bf16),
+        ((BL, 3 * BL), bf16),
         ((STEPS, 2, RD, 128), f32),
         ((STEPS, 2, RD, 128), f32),
         ((STEPS, 2, RD, HC), f32),
@@ -444,125 +568,26 @@
         functools.partial(adi_kernel, (K, Q, C, RD, NC, BL)),
         out_shape=(
             jax.ShapeDtypeStruct((RD, NC), f32),
-            jax.ShapeDtypeStruct((2, RD, C * NC), f32),
+            jax.ShapeDtypeStruct((2, pins), f32),
         ),
-        in_specs=[vmem] * 5,
+        in_specs=[pl.BlockSpec(memory_space=pl.ANY)] * 8,
         out_specs=(vmem, vmem),
         scratch_shapes=[pltpu.VMEM(shape, dtype) for shape, dtype in shapes]
-        + [pltpu.SemaphoreType.DMA((15,)), pltpu.SemaphoreType.DMA((15,))],
+        + [pltpu.SemaphoreType.DMA((n,)) for n in (15, 15, 8)],
         compiler_params=pltpu.CompilerParams(
             collective_id=0, has_side_effects=True, vmem_limit_bytes=48 << 20
         ),
         name="adi",
-    )(part, capacity, blockage, row_blocks, col_blocks)
-
-
-def pin_tables(block_rows, block_cols, row_near, row_far, col_near, col_far, rows_dev, hi_count):
-    block_size = block_rows.shape[0]
-    zero_value = jnp.zeros((), jnp.bfloat16)
-    row_index = lax.broadcasted_iota(jnp.int32, (block_size, rows_dev), 1)
-    row_table = jnp.where(
-        row_index == block_rows[:, None], row_near[:, None], zero_value
-    ) + jnp.where(row_index == block_rows[:, None] + 1, row_far[:, None], zero_value)
-    high_index = lax.broadcasted_iota(jnp.int32, (block_size, 1, hi_count), 2)
-    low_index = lax.broadcasted_iota(jnp.int32, (block_size, 128), 1)
-    bin_tables = []
-    lane_tables = []
-    for offset, factor in ((0, col_near), (1, col_far)):
-        column = block_cols + offset
-        high_part = column // 128
-        low_part = column - high_part * 128
-        chosen = (high_index == high_part[:, None, None]).astype(jnp.bfloat16)
-        bin_tables.append((row_table[:, :, None] * chosen).reshape(block_size, rows_dev * hi_count))
-        lane_tables.append(jnp.where(low_index == low_part[:, None], factor[:, None], zero_value))
-    return (jnp.concatenate(bin_tables, 0), jnp.concatenate(lane_tables, 0))
-
-
-def pin_factors(pin_rows, pin_cols, row_near, row_far, col_near, col_far):
-    block_size = min(2048, pin_rows.shape[0])
-    return (
-        block_size,
-        tuple(
-            (
-                item.reshape(-1, block_size)
-                for item in (pin_rows, pin_cols, row_near, row_far, col_near, col_far)
-            )
-        ),
+    )(
+        pin_rows.reshape(chunks, 128),
+        pin_cols.reshape(chunks, 128),
+        pin_fracs,
+        pin_weights.reshape(chunks, 128),
+        capacity,
+        blockage,
+        row_blocks,
+        col_blocks,
     )
-
-
-def splat(pin_rows, pin_cols, pin_fracs, pin_weights, rows_dev, hi_count):
-    near_y = 1.0 - pin_fracs[0]
-    near_x = 1.0 - pin_fracs[1]
-    block_size, pieces = pin_factors(
-        pin_rows,
-        pin_cols,
-        (pin_weights * near_y).astype(jnp.bfloat16),
-        (pin_weights * pin_fracs[0]).astype(jnp.bfloat16),
-        near_x.astype(jnp.bfloat16),
-        pin_fracs[1].astype(jnp.bfloat16),
-    )
-
-    def add_block(total, block):
-        bins, lane_table = pin_tables(
-            block[0], block[1], block[2], block[3], block[4], block[5], rows_dev, hi_count
-        )
-        part_sum = lax.dot_general(
-            bins, lane_table, (((0,), (0,)), ((), ())), preferred_element_type=jnp.float32
-        )
-        return (total + part_sum, None)
-
-    total, unused = lax.scan(add_block, jnp.zeros((rows_dev * hi_count, 128), jnp.float32), pieces)
-    return total.reshape(rows_dev, hi_count * 128)
-
-
-def interpolate(pin_rows, pin_cols, pin_fracs, velocity_y, velocity_x, rows_dev, hi_count):
-    stacked = jnp.concatenate(
-        [
-            velocity_y.reshape(rows_dev * hi_count, 128),
-            velocity_x.reshape(rows_dev * hi_count, 128),
-        ],
-        1,
-    )
-    npins = pin_rows.shape[0]
-    block_size, pieces = pin_factors(
-        pin_rows,
-        pin_cols,
-        (1.0 - pin_fracs[0]).astype(jnp.bfloat16),
-        pin_fracs[0].astype(jnp.bfloat16),
-        (1.0 - pin_fracs[1]).astype(jnp.bfloat16),
-        pin_fracs[1].astype(jnp.bfloat16),
-    )
-
-    def one_block(carry, block):
-        bins, lane_table = pin_tables(
-            block[0], block[1], block[2], block[3], block[4], block[5], rows_dev, hi_count
-        )
-        sampled = jnp.dot(bins, stacked, preferred_element_type=jnp.float32)
-        lane_values = lane_table.astype(jnp.float32)
-        both_y = jnp.sum(sampled[:, :128] * lane_values, axis=1)
-        both_x = jnp.sum(sampled[:, 128:] * lane_values, axis=1)
-        result = jnp.stack(
-            [both_y[:block_size] + both_y[block_size:], both_x[:block_size] + both_x[block_size:]]
-        )
-        return (carry, result)
-
-    unused, outputs = lax.scan(one_block, jnp.zeros((), jnp.float32), pieces)
-    return jnp.transpose(outputs, (1, 0, 2)).reshape(2, npins)
-
-
-def local(pin_rows, pin_cols, pin_fracs, pin_weights, capacity, blockage, row_blocks, col_blocks):
-    rows_dev, cols_dev = capacity.shape
-    cells = lax.axis_size("cells")
-    hi_count = cols_dev * cells // 128
-    part = splat(pin_rows, pin_cols, pin_fracs, pin_weights, rows_dev, hi_count)
-    part = jnp.transpose(part.reshape(rows_dev, cells, cols_dev), (1, 0, 2))
-    current, velocity = diffuse(part, capacity, blockage, row_blocks, col_blocks)
-    velocity = velocity.astype(bf16)
-    pin_velocity = interpolate(
-        pin_rows, pin_cols, pin_fracs, velocity[0], velocity[1], rows_dev, hi_count
-    )
-    return (current, pin_velocity)
 
 
 def solution(mesh):
@@ -577,7 +602,7 @@
         P(),
     )
     return jax.shard_map(
-        local,
+        diffuse,
         mesh=mesh,
         in_specs=placed,
         out_specs=(P("strip", "cells"), P(None, ("strip", "cells"))),

time: 86.3 us -> 80.9 us (0.937)
  other arithmetic: 6.64 us -> 0 us
  local copies, waits for them, and re-layouts: 4.19 us -> 7.44 us
  matrix products: 2.17 us -> 0 us
    unnamed x11 -> x18, local copies, waits for them, and re-layouts: 0.63 us -> 7.44 us
    select_n x10 -> x0, other arithmetic: 3.27 us -> none  [the longest x8 3.24 us: pin_tables(): jnp.where(low_index == low_part[:, None], factor[:, None], zero_value)]
    dot_general x4 -> x0, matrix products: 2.17 us -> none  [the longest x2 1.48 us: one_block(): sampled = jnp.dot(bins, stacked, preferred_element_type=jnp.float32)]
    convert_element_type x11 -> x0, other arithmetic: 1.93 us -> none  [the longest x1 1.01 us: interpolate(): pin_fracs[0].astype(jnp.bfloat16)]
    reshape x4 -> x0, local copies, waits for them, and re-layouts: 1.49 us -> none  [pin_factors(): item.reshape(-1, block_size)]
    reduce_sum x2 -> x0, other arithmetic: 0.95 us -> none  [one_block(): both_y = jnp.sum(sampled[:, :128] * lane_values, axis=1)]
where the time goes in v2:
time: 80.9 us; the launch traced here: 80.3 us
  Pallas kernels  72.2 us (89%)
  local copies, waits for them, and re-layouts  7.44 us (9%)
    pallas_call x1, Pallas kernels, diffuse(): pl.pallas_call(functools.partial(adi_kernel, (K, Q, C, RD, NC, BL)), out_...  72.2 us
    unnamed x18, local copies, waits for them, and re-layouts  7.44 us

profile of v2, /device:TPU:1, one launch (start us, length us, event | category | flops | bytes accessed | tf_op | source)
XLA Modules:
  0.0 80.3 jit_solution(3869614676511284558)
XLA Ops:
  0.6 0.0 copy-start
  0.6 1.0 %copy-done = f32[5,128,128]{2,1,0:T(8,128)S(1)} copy-done((f32[5,128,128]{2,1,0:T(8,128)S(1)}, f32[5,128,128]{2,1,0:T(8,128)}, u32[]{:S(2)}) %copy-start) | copy-done | bytes 327704
  1.6 0.0 copy-start.1
  1.6 0.9 %copy-done.1 = f32[4,128,128]{2,1,0:T(8,128)S(1)} copy-done((f32[4,128,128]{2,1,0:T(8,128)S(1)}, f32[4,128,128]{2,1,0:T(8,128)}, u32[]{:S(2)}) %copy-start.1) | copy-done | bytes 262168
  2.6 0.0 copy-start.2
  2.6 0.8 copy-done.2
  3.3 0.0 copy-start.3
  3.3 0.7 copy-done.3
  4.0 0.0 copy-start.4
  4.0 0.7 copy-done.4
  4.8 0.0 copy-start.5
  4.8 0.7 copy-done.5
  5.5 0.0 copy-start.6
  5.5 0.7 copy-done.6
  6.2 0.0 copy-start.7
  6.2 0.7 copy-done.7
  6.9 72.2 %adi.1 = (f32[4,640]{1,0:T(4,128)S(1)}, f32[2,4096]{1,0:T(2,128)S(1)}) custom-call(s32[32,128]{1,0:T(8,128)S(1)} %bitcast.3, s32[32,128]{1,0:T(8,128)S(1)} %bitcast.4, f32[2,4096]{1,0:T(2,128)S(1)} %copy-done.2, f32[32,128]{1,0:T(8,128)S(1)} %bitcast.5, s32[4,640]{1,0:T(4,128)S(1)} %copy-done.6, f32[4,640]{1,0:T(4,128)S(1)} %copy-done.7, ...), custom_call_target="tpu_custom_call" | custom-call | tf_op jit(solution)/shard_map/adi/pallas_call | solution.py:567
  79.1 0.6 copy.12
  79.7 0.6 copy.13
Async XLA Ops:
  0.6 1.0 %copy-start = (f32[5,128,128]{2,1,0:T(8,128)S(1)}, f32[5,128,128]{2,1,0:T(8,128)}, u32[]{:S(2)}) copy-start(f32[5,128,128]{2,1,0:T(8,128)} %rowb_hbm.1) | copy-start | bytes 983044
  1.6 0.9 %copy-start.1 = (f32[4,128,128]{2,1,0:T(8,128)S(1)}, f32[4,128,128]{2,1,0:T(8,128)}, u32[]{:S(2)}) copy-start(f32[4,128,128]{2,1,0:T(8,128)} %colb_hbm.1) | copy-start | bytes 786436
  2.6 0.8 copy-start.2
  3.3 0.7 copy-start.3
  4.0 0.7 copy-start.4
  4.8 0.7 copy-start.5
  5.5 0.7 copy-start.6
  6.2 0.7 copy-start.7

commit v3 on v2

--- a/solution.py
+++ b/solution.py
@@ -11,6 +11,7 @@
 STEPS = 2
 coupling = 2.0
 floor_level = 0.5
+w_steps = 8191.0
 f32 = jnp.float32
 bf16 = jnp.bfloat16
 
@@ -214,8 +215,9 @@
             part_ref[c, :, 128 * n : 128 * (n + 1)] = bin_sums[RD * tile : RD * (tile + 1), :]
 
     weights = cap_ref[...].astype(f32) * (1.0 - blk_ref[...])
-    w_send[0] = weights[:, :HC]
-    w_send[1] = weights[:, cut:]
+    whole = jnp.round(weights * w_steps).astype(jnp.int32).astype(jnp.int16)
+    w_send[0] = whole[:, :HC]
+    w_send[1] = whole[:, cut:]
     w_plane[place] = w_send[half]
     wedge_send[0] = weights[:1]
     wedge_send[1] = weights[RD - 1 :]
@@ -356,7 +358,8 @@
         if step == 0:
             arrived(3, w_plane.at[0 : Q - 1])
             for i in range(Q):
-                w_block[RD * i : RD * (i + 1), :] = w_plane[i]
+                stepped = w_plane[i].astype(jnp.int32).astype(f32)
+                w_block[RD * i : RD * (i + 1), :] = stepped * (1.0 / w_steps)
             padded[0:8, :] = jnp.zeros((8, HC), f32)
             padded[BL + 8 :, :] = jnp.zeros((8, HC), f32)
             for side, column in ((0, 0), (1, BL - 1)):
@@ -539,8 +542,8 @@
         ((2, C, 1, NC), f32),
         ((2, 1, NC), f32),
         ((2, 1, NC), f32),
-        ((2, RD, HC), f32),
-        ((Q, RD, HC), f32),
+        ((2, RD, HC), jnp.int16),
+        ((Q, RD, HC), jnp.int16),
         ((BL, HC), f32),
         ((NB, 128, 384), bf16),
         ((BL, 3 * BL), bf16),
@@ -570,12 +573,12 @@
             jax.ShapeDtypeStruct((RD, NC), f32),
             jax.ShapeDtypeStruct((2, pins), f32),
         ),
-        in_specs=[pl.BlockSpec(memory_space=pl.ANY)] * 8,
+        in_specs=[pl.BlockSpec(memory_space=pltpu.HBM)] * 8,
         out_specs=(vmem, vmem),
         scratch_shapes=[pltpu.VMEM(shape, dtype) for shape, dtype in shapes]
         + [pltpu.SemaphoreType.DMA((n,)) for n in (15, 15, 8)],
         compiler_params=pltpu.CompilerParams(
-            collective_id=0, has_side_effects=True, vmem_limit_bytes=48 << 20
+            collective_id=0, has_side_effects=True
         ),
         name="adi",
     )(

time: 80.9 us -> 75 us (0.927)
  local copies, waits for them, and re-layouts: 7.44 us -> 2.68 us
    unnamed x18 -> x2, local copies, waits for them, and re-layouts: 7.44 us -> 2.68 us
where the time goes in v3:
time: 75 us; the launch traced here: 74.8 us
  Pallas kernels  71.4 us (95%)
  local copies, waits for them, and re-layouts  2.68 us (4%)
    pallas_call x1, Pallas kernels, diffuse(): pl.pallas_call(functools.partial(adi_kernel, (K, Q, C, RD, NC, BL)), out_...  71.4 us
    unnamed x2, local copies, waits for them, and re-layouts  2.68 us

profile of v3, /device:TPU:1, one launch (start us, length us, event | category | flops | bytes accessed | tf_op | source)
XLA Modules:
  0.0 74.8 jit_solution(3284615825918331553)
XLA Ops:
  0.6 71.4 %adi.1 = (f32[4,640]{1,0:T(4,128)}, f32[2,4096]{1,0:T(2,128)}) custom-call(s32[32,128]{1,0:T(8,128)} %bitcast.3, s32[32,128]{1,0:T(8,128)} %bitcast.4, f32[2,4096]{1,0:T(2,128)} %fracs_hbm.1, f32[32,128]{1,0:T(8,128)} %bitcast.5, s32[4,640]{1,0:T(4,128)} %cap_hbm.1, f32[4,640]{1,0:T(4,128)} %blk_hbm.1, f32[5,128,128]{2,1,0:T(8,128)} %rowb_hbm.1, ...), custom_call_target="tpu_custom_call" | custom-call | tf_op jit(solution)/shard_map/adi/pallas_call | solution.py:570
  72.1 1.3 %copy.12 = f32[4,640]{1,0:T(4,128)} copy(f32[4,640]{1,0:T(4,128)} %get-tuple-element.4) | data formatting | bytes 20480
  73.4 1.4 %copy.13 = f32[2,4096]{1,0:T(2,128)} copy(f32[2,4096]{1,0:T(2,128)} %get-tuple-element.5) | data formatting | bytes 65536

commit v4 on v3

--- a/solution.py
+++ b/solution.py
@@ -21,14 +21,14 @@
     return high, (values - high.astype(f32)).astype(bf16)
 
 
-def row_product(values, blocks_ref):
+def row_product(values, blocks_ref, first=0):
     pieces = []
-    for n in range(blocks_ref.shape[0]):
+    for n in range(values.shape[1] // 128):
         high, low = exact_parts(values[:, 128 * n : 128 * (n + 1)])
         pieces.append(
             lax.dot_general(
                 jnp.concatenate([high, low, high], axis=1),
-                blocks_ref[n],
+                blocks_ref[first + n],
                 (((1,), (1,)), ((), ())),
                 preferred_element_type=f32,
             )
@@ -87,6 +87,10 @@
     field_send,
     field_plane,
     field_block,
+    inflow_send,
+    inflow_plane,
+    inflow_block,
+    waves,
     padded,
     answer_send,
     answer_near,
@@ -244,7 +248,6 @@
     high, low = exact_parts(colb_ref[...])
     colb_parts[...] = jnp.concatenate([high, high, low], axis=1)
 
-    end = lax.broadcasted_iota(jnp.int32, (RD, HC), 1)
 
     def along_inside(values):
         left = pltpu.roll(values, 1, 1)
@@ -252,6 +255,16 @@
         spot = lax.broadcasted_iota(jnp.int32, values.shape, 1)
         left = jnp.where(spot == 0, jnp.where(first_cell, values, 0.0), left)
         right = jnp.where(spot == NC - 1, jnp.where(last_cell, values, 0.0), right)
+        return 2.0 * values - left - right
+
+    def along_half(values):
+        left = pltpu.roll(values, 1, 1)
+        right = pltpu.roll(values, HC - 1, 1)
+        spot = lax.broadcasted_iota(jnp.int32, values.shape, 1)
+        at_left = jnp.logical_and(half == 0, first_cell)
+        at_right = jnp.logical_and(half == 1, last_cell)
+        left = jnp.where(spot == 0, jnp.where(at_left, values, 0.0), left)
+        right = jnp.where(spot == HC - 1, jnp.where(at_right, values, 0.0), right)
         return 2.0 * values - left - right
 
     weights_two = jnp.concatenate([weights, weights], axis=0)
@@ -328,6 +341,11 @@
         send(group, rim_send.at[step, 0], rim_recv.at[step, 1], at(strip, (cell + C - 1) % C))
         send(group, rim_send.at[step, 1], rim_recv.at[step, 0], at(strip, (cell + 1) % C))
 
+        field_send[step, 0] = iterate[:, :HC]
+        field_send[step, 1] = iterate[:, cut:]
+        field_plane[step, place] = field_send[step, half]
+        for peer, other_half in plane_peers:
+            send(group + 2, field_send.at[step, other_half], field_plane.at[step, place], peer)
         arrived(group, rim_recv.at[step])
         edges = []
         for side in range(2):
@@ -344,17 +362,25 @@
             edges.append(theirs)
         left_in = [jnp.where(first_cell, 0.0, e) for e in edges[0]]
         right_in = [jnp.where(last_cell, 0.0, e) for e in edges[1]]
-        for i in range(SWEEPS):
-            iterate = iterate + (
-                pulses[SWEEPS - 1 - i][:RD] * left_in[i] + pulses[SWEEPS - 1 - i][RD:] * right_in[i]
-            )
         halo_left = jnp.where(first_cell, iterate[:, :1], left_in[SWEEPS])
         halo_right = jnp.where(last_cell, iterate[:, NC - 1 :], right_in[SWEEPS])
-        field_send[step, 0] = jnp.where(end == HC - 1, halo_left, iterate[:, :HC])
-        field_send[step, 1] = jnp.where(end == 0, halo_right, iterate[:, cut:])
-        field_plane[step, place] = field_send[step, half]
+        far_left = pulses[1][:RD, cut - 1 : cut] * left_in[0]
+        far_right = pulses[1][RD:, HC : HC + 1] * right_in[0]
+        for h, entries in (
+            (0, left_in[:SWEEPS] + [halo_left, far_right]),
+            (1, right_in[:SWEEPS] + [halo_right, far_left]),
+        ):
+            message = jnp.zeros((RD, 128), f32)
+            for i, entry in enumerate(entries):
+                message = jnp.where(small == i, entry, message)
+            packed = message[:1]
+            for r in range(1, RD):
+                packed = packed + pltpu.roll(message, 8 * r, 1)[r : r + 1]
+            inflow_send[step, h] = packed
+        inflow_plane[step, place] = inflow_send[step, half]
         for peer, other_half in plane_peers:
-            send(group + 2, field_send.at[step, other_half], field_plane.at[step, place], peer)
+            send(15 + step, inflow_send.at[step, other_half], inflow_plane.at[step, place], peer)
+
         if step == 0:
             arrived(3, w_plane.at[0 : Q - 1])
             for i in range(Q):
@@ -380,6 +406,19 @@
             for peer in plane_cross:
                 send(5, still_send, still_recv.at[slot], peer)
             send(9, answer_send, answer_near.at[half], partner)
+
+            place_in_half = lax.broadcasted_iota(jnp.int32, (8, HC), 1)
+            outer = jnp.where(half == 0, 0, HC - 1)
+            unit = jnp.where(place_in_half == outer, coupling, 0.0)
+            wave = row_product(unit, rowb_parts, 2 * half)[:1]
+            wave = jnp.broadcast_to(wave, (BL, HC))
+            waves[0] = wave
+            for m in range(1, SWEEPS):
+                back = w_block[...] * wave + coupling * along_half(wave)
+                wave = wave - row_product(back, rowb_parts, 2 * half)
+                waves[m] = wave
+            unit = jnp.where(place_in_half == HC - 1 - outer, coupling, 0.0)
+            inner_wave = row_product(unit, rowb_parts, 2 * half)[:1]
         else:
 
             def prepare(i, carry):
@@ -394,7 +433,22 @@
         for i in range(Q):
             field_block[RD * i : RD * (i + 1), :] = field_plane[step, i]
 
-        start = field_block[...]
+        arrived(15 + step, inflow_plane.at[step, 0 : Q - 1])
+        for i in range(Q):
+            inflow_block[RD * i : RD * (i + 1), :] = jnp.broadcast_to(
+                inflow_plane[step, i], (RD, 128)
+            )
+        packed = inflow_block[...]
+        turn = lax.broadcasted_iota(jnp.int32, (BL, 128), 0) % RD
+        entries = packed
+        for r in range(1, RD):
+            entries = jnp.where(turn == r, pltpu.roll(packed, 128 - 8 * r, 1), entries)
+        start = field_block[...] + inner_wave * entries[:, SWEEPS + 1 : SWEEPS + 2]
+        for i in range(SWEEPS):
+            start = start + waves[SWEEPS - 1 - i] * entries[:, i : i + 1]
+        spot = lax.broadcasted_iota(jnp.int32, (BL, HC), 1)
+        unused = jnp.where(half == 0, HC - 1, 0)
+        start = jnp.where(spot == unused, entries[:, SWEEPS : SWEEPS + 1], start)
         beside = pltpu.roll(start, 1, 1) + pltpu.roll(start, HC - 1, 1)
         middle = w_block[...] * start - coupling * (2.0 * start - beside)
         iterate = start
@@ -552,6 +606,10 @@
         ((STEPS, 2, RD, HC), f32),
         ((STEPS, Q, RD, HC), f32),
         ((BL, HC), f32),
+        ((STEPS, 2, 1, 128), f32),
+        ((STEPS, Q, 1, 128), f32),
+        ((BL, 128), f32),
+        ((SWEEPS, BL, HC), f32),
         ((BL + 16, HC), f32),
         ((SWEEPS, 2, 8, HC), f32),
         ((2, SWEEPS, 2, 8, HC), f32),
@@ -567,7 +625,7 @@
         ((8, NC), f32),
         ((C, 8, NC), f32),
     ]
-    return pl.pallas_call(
+    results = pl.pallas_call(
         functools.partial(adi_kernel, (K, Q, C, RD, NC, BL)),
         out_shape=(
             jax.ShapeDtypeStruct((RD, NC), f32),
@@ -576,7 +634,7 @@
         in_specs=[pl.BlockSpec(memory_space=pltpu.HBM)] * 8,
         out_specs=(vmem, vmem),
         scratch_shapes=[pltpu.VMEM(shape, dtype) for shape, dtype in shapes]
-        + [pltpu.SemaphoreType.DMA((n,)) for n in (15, 15, 8)],
+        + [pltpu.SemaphoreType.DMA((n,)) for n in (17, 17, 8)],
         compiler_params=pltpu.CompilerParams(
             collective_id=0, has_side_effects=True
         ),
@@ -591,6 +649,25 @@
         row_blocks,
         col_blocks,
     )
+    return pl.pallas_call(
+        hand_over,
+        out_shape=[jax.ShapeDtypeStruct(r.shape, r.dtype) for r in results],
+        in_specs=[pl.BlockSpec(memory_space=pl.ANY)] * 2,
+        out_specs=[pl.BlockSpec(memory_space=pl.ANY)] * 2,
+        scratch_shapes=[pltpu.SemaphoreType.DMA((2,))],
+        name="hand_over",
+    )(*results)
+
+
+def hand_over(first, second, first_out, second_out, sems):
+    copies = [
+        pltpu.make_async_copy(first, first_out, sems.at[0]),
+        pltpu.make_async_copy(second, second_out, sems.at[1]),
+    ]
+    for copy in copies:
+        copy.start()
+    for copy in copies:
+        copy.wait()
 
 
 def solution(mesh):

time: 75 us -> 76.3 us (1.017)
  Pallas kernels: 71.4 us -> 75.5 us
  local copies, waits for them, and re-layouts: 2.68 us -> 0 us
    unnamed x2 -> x0, local copies, waits for them, and re-layouts: 2.68 us -> none
    pallas_call x0 -> x1, Pallas kernels: none -> 2.42 us  [diffuse(): pl.pallas_call(hand_over, out_shape=[jax.ShapeDtypeStruct(r.shape, r.dtyp...]
    pallas_call x1, Pallas kernels: 71.4 us -> 73.1 us  [diffuse(): pl.pallas_call(functools.partial(adi_kernel, (K, Q, C, RD, NC, BL)), out_...]
where the time goes in v4:
time: 76.3 us; the launch traced here: 76.2 us
  Pallas kernels  75.5 us (99%)
    pallas_call x1, Pallas kernels, diffuse(): pl.pallas_call(functools.partial(adi_kernel, (K, Q, C, RD, NC, BL)), out_...  73.1 us
    pallas_call x1, Pallas kernels, diffuse(): pl.pallas_call(hand_over, out_shape=[jax.ShapeDtypeStruct(r.shape, r.dtyp...  2.42 us

profile of v4, /device:TPU:1, one launch (start us, length us, event | category | flops | bytes accessed | tf_op | source)
XLA Modules:
  0.0 76.2 jit_solution(894829259949069511)
XLA Ops:
  0.6 73.1 %adi.1 = (f32[4,640]{1,0:T(4,128)}, f32[2,4096]{1,0:T(2,128)}) custom-call(s32[32,128]{1,0:T(8,128)} %bitcast.3, s32[32,128]{1,0:T(8,128)} %bitcast.4, f32[2,4096]{1,0:T(2,128)} %fracs_hbm.1, f32[32,128]{1,0:T(8,128)} %bitcast.5, s32[4,640]{1,0:T(4,128)} %cap_hbm.1, f32[4,640]{1,0:T(4,128)} %blk_hbm.1, f32[5,128,128]{2,1,0:T(8,128)} %rowb_hbm.1, ...), custom_call_target="tpu_custom_call" | custom-call | tf_op jit(solution)/shard_map/adi/pallas_call | solution.py:628
  73.7 2.4 %hand_over.1 = (f32[4,640]{1,0:T(4,128)}, f32[2,4096]{1,0:T(2,128)}) custom-call(f32[4,640]{1,0:T(4,128)} %get-tuple-element.4.first, f32[2,4096]{1,0:T(2,128)} %get-tuple-element.5.second), custom_call_target="tpu_custom_call" | custom-call | tf_op jit(solution)/shard_map/hand_over/pallas_call | solution.py:652

commit v5 on v3

--- a/solution.py
+++ b/solution.py
@@ -377,9 +377,6 @@
                     still_send[m, side, 0:1, :] = answer[:1]
                     still_send[m, side, 1:2, :] = answer[BL - 1 :]
             still_recv[slot] = still_send[...]
-            for peer in plane_cross:
-                send(5, still_send, still_recv.at[slot], peer)
-            send(9, answer_send, answer_near.at[half], partner)
         else:
 
             def prepare(i, carry):
@@ -391,6 +388,10 @@
             lax.fori_loop(0, chunks, prepare, 0, unroll=2)
 
         arrived(group + 2, field_plane.at[step, 0 : Q - 1])
+        if step == 0:
+            send(9, answer_send, answer_near.at[half], partner)
+            for peer in plane_cross:
+                send(5, still_send, still_recv.at[slot], peer)
         for i in range(Q):
             field_block[RD * i : RD * (i + 1), :] = field_plane[step, i]
 
@@ -567,7 +568,7 @@
         ((8, NC), f32),
         ((C, 8, NC), f32),
     ]
-    return pl.pallas_call(
+    results = pl.pallas_call(
         functools.partial(adi_kernel, (K, Q, C, RD, NC, BL)),
         out_shape=(
             jax.ShapeDtypeStruct((RD, NC), f32),
@@ -591,6 +592,18 @@
         row_blocks,
         col_blocks,
     )
+    return pl.pallas_call(
+        hand_over,
+        out_shape=[jax.ShapeDtypeStruct(r.shape, r.dtype) for r in results],
+        in_specs=[vmem] * 2,
+        out_specs=[vmem] * 2,
+        name="hand_over",
+    )(*results)
+
+
+def hand_over(first, second, first_out, second_out):
+    first_out[...] = first[...]
+    second_out[...] = second[...]
 
 
 def solution(mesh):

time: 75 us -> 75.9 us (1.012)
  Pallas kernels: 71.4 us -> 75 us
  local copies, waits for them, and re-layouts: 2.68 us -> 0 us
    unnamed x2 -> x0, local copies, waits for them, and re-layouts: 2.68 us -> none
    pallas_call x1, Pallas kernels: 71.4 us -> 73.6 us  [diffuse(): pl.pallas_call(functools.partial(adi_kernel, (K, Q, C, RD, NC, BL)), out_...]
    pallas_call x0 -> x1, Pallas kernels: none -> 1.4 us  [diffuse(): pl.pallas_call(hand_over, out_shape=[jax.ShapeDtypeStruct(r.shape, r.dtyp...]
where the time goes in v5:
time: 75.9 us; the launch traced here: 75.6 us
  Pallas kernels  75 us (99%)
    pallas_call x1, Pallas kernels, diffuse(): pl.pallas_call(functools.partial(adi_kernel, (K, Q, C, RD, NC, BL)), out_...  73.6 us

profile of v5, /device:TPU:1, one launch (start us, length us, event | category | flops | bytes accessed | tf_op | source)
XLA Modules:
  0.0 75.6 jit_solution(10054298833491836319)
XLA Ops:
  0.6 73.6 %adi.1 = (f32[4,640]{1,0:T(4,128)}, f32[2,4096]{1,0:T(2,128)}) custom-call(s32[32,128]{1,0:T(8,128)} %bitcast.3, s32[32,128]{1,0:T(8,128)} %bitcast.4, f32[2,4096]{1,0:T(2,128)} %fracs_hbm.1, f32[32,128]{1,0:T(8,128)} %bitcast.5, s32[4,640]{1,0:T(4,128)} %cap_hbm.1, f32[4,640]{1,0:T(4,128)} %blk_hbm.1, f32[5,128,128]{2,1,0:T(8,128)} %rowb_hbm.1, ...), custom_call_target="tpu_custom_call" | custom-call | tf_op jit(solution)/shard_map/adi/pallas_call | solution.py:571
  74.2 1.4 %hand_over.1 = (f32[4,640]{1,0:T(4,128)}, f32[2,4096]{1,0:T(2,128)}) custom-call(f32[4,640]{1,0:T(4,128)} %get-tuple-element.4.first, f32[2,4096]{1,0:T(2,128)} %get-tuple-element.5.second), custom_call_target="tpu_custom_call" | custom-call | tf_op jit(solution)/shard_map/hand_over/pallas_call | solution.py:595

commit v6 on v5

--- a/solution.py
+++ b/solution.py
@@ -377,21 +377,23 @@
                     still_send[m, side, 0:1, :] = answer[:1]
                     still_send[m, side, 1:2, :] = answer[BL - 1 :]
             still_recv[slot] = still_send[...]
-        else:
-
-            def prepare(i, carry):
-                down, across, index, lane = pins_of(i)
-                look[i] = table(index, rounded(1.0 - down), rounded(down), 128).astype(bf16)
-                spread[i] = table(lane, rounded(1.0 - across), rounded(across), 136)
-                return carry
-
-            lax.fori_loop(0, chunks, prepare, 0, unroll=2)
-
-        arrived(group + 2, field_plane.at[step, 0 : Q - 1])
-        if step == 0:
-            send(9, answer_send, answer_near.at[half], partner)
             for peer in plane_cross:
                 send(5, still_send, still_recv.at[slot], peer)
+            send(9, answer_send, answer_near.at[half], partner)
+        else:
+
+            def prepare(i, carry):
+                for k in range(2):
+                    down, across, index, lane = pins_of(2 * i + k)
+                    part = slice(128 * k, 128 * (k + 1))
+                    nearer, farther = rounded(1.0 - down), rounded(down)
+                    look[i, :, part] = table(index, nearer, farther, 128).astype(bf16)
+                    spread[i, :, part] = table(lane, rounded(1.0 - across), rounded(across), 136)
+                return carry
+
+            lax.fori_loop(0, chunks // 2, prepare, 0)
+
+        arrived(group + 2, field_plane.at[step, 0 : Q - 1])
         for i in range(Q):
             field_block[RD * i : RD * (i + 1), :] = field_plane[step, i]
 
@@ -503,11 +505,11 @@
         across = spread[i]
         out_y = jnp.sum(sampled[:136] * across, axis=0, keepdims=True)
         out_x = jnp.sum(sampled[136:] * across, axis=0, keepdims=True)
-        span = pl.ds(pl.multiple_of(128 * i, 128), 128)
+        span = pl.ds(pl.multiple_of(256 * i, 256), 256)
         pinv_ref[:, span] = jnp.concatenate([out_y, out_x], axis=0)
         return carry
 
-    lax.fori_loop(0, chunks, sample, 0, unroll=4)
+    lax.fori_loop(0, chunks // 2, sample, 0, unroll=4)
     for group, span in sent:
         pltpu.make_async_copy(span, span, send_sem.at[group]).wait()
 
@@ -535,8 +537,8 @@
         ((BL, BL), f32),
         ((bins, 128), f32),
         ((C, RD, NC), f32),
-        ((chunks, 128, 128), bf16),
-        ((chunks, 136, 128), f32),
+        ((chunks // 2, 128, 256), bf16),
+        ((chunks // 2, 136, 256), f32),
         ((2, 128, 128), f32),
         ((2, C, 1, NC), f32),
         ((C, RD, NC), f32),
@@ -578,9 +580,7 @@
         out_specs=(vmem, vmem),
         scratch_shapes=[pltpu.VMEM(shape, dtype) for shape, dtype in shapes]
         + [pltpu.SemaphoreType.DMA((n,)) for n in (15, 15, 8)],
-        compiler_params=pltpu.CompilerParams(
-            collective_id=0, has_side_effects=True
-        ),
+        compiler_params=pltpu.CompilerParams(collective_id=0, has_side_effects=True),
         name="adi",
     )(
         pin_rows.reshape(chunks, 128),

time: 75.9 us -> 72.6 us (0.957)
  Pallas kernels: 75 us -> 71.6 us
    pallas_call x1, Pallas kernels: 73.6 us -> 70.2 us  [diffuse(): pl.pallas_call(functools.partial(adi_kernel, (K, Q, C, RD, NC, BL)), out_...]
where the time goes in v6:
time: 72.6 us; the launch traced here: 72.3 us
  Pallas kernels  71.6 us (99%)
    pallas_call x1, Pallas kernels, diffuse(): pl.pallas_call(functools.partial(adi_kernel, (K, Q, C, RD, NC, BL)), out_...  70.2 us

profile of v6, /device:TPU:1, one launch (start us, length us, event | category | flops | bytes accessed | tf_op | source)
XLA Modules:
  0.0 72.3 jit_solution(17813446915330181117)
XLA Ops:
  0.6 70.2 %adi.1 = (f32[4,640]{1,0:T(4,128)}, f32[2,4096]{1,0:T(2,128)}) custom-call(s32[32,128]{1,0:T(8,128)} %bitcast.3, s32[32,128]{1,0:T(8,128)} %bitcast.4, f32[2,4096]{1,0:T(2,128)} %fracs_hbm.1, f32[32,128]{1,0:T(8,128)} %bitcast.5, s32[4,640]{1,0:T(4,128)} %cap_hbm.1, f32[4,640]{1,0:T(4,128)} %blk_hbm.1, f32[5,128,128]{2,1,0:T(8,128)} %rowb_hbm.1, ...), custom_call_target="tpu_custom_call" | custom-call | tf_op jit(solution)/shard_map/adi/pallas_call | solution.py:573
  70.9 1.4 %hand_over.1 = (f32[4,640]{1,0:T(4,128)}, f32[2,4096]{1,0:T(2,128)}) custom-call(f32[4,640]{1,0:T(4,128)} %get-tuple-element.4.first, f32[2,4096]{1,0:T(2,128)} %get-tuple-element.5.second), custom_call_target="tpu_custom_call" | custom-call | tf_op jit(solution)/shard_map/hand_over/pallas_call | solution.py:595

commit v7 on v6

--- a/solution.py
+++ b/solution.py
@@ -137,6 +137,11 @@
         at(((plane + dk) % K) * Q + place + dz * (2 - 4 * half), cell) for dk, dz in shifts
     ]
     slot = 2 * plane + half
+    plane_next = [
+        at(((plane + dk) % K) * Q + place + dz * (2 - 4 * half), cell)
+        for dk, dz in shifts
+        if dk in (1, K - 1)
+    ]
     row_peers = [at(s, (cell + d) % C) for s in (above_strip, below_strip) for d in range(C)]
 
     barrier = pltpu.get_barrier_semaphore()
@@ -402,13 +407,26 @@
         middle = w_block[...] * start - coupling * (2.0 * start - beside)
         iterate = start
         for j in range(SWEEPS + 1):
+            if j == SWEEPS:
+                for peer in plane_cross:
+                    send(
+                        group + 3,
+                        tops_send.at[step, 0:SWEEPS],
+                        tops_recv.at[step, slot, 0:SWEEPS],
+                        peer,
+                    )
             if j > 0:
                 left_over = middle - (w_block[...] * iterate + coupling * clamp_rows(iterate))
                 iterate = iterate + col_product(colb_parts, left_over)
             tops_send[step, j, 0:1, :] = iterate[:1]
             tops_send[step, j, 1:2, :] = iterate[BL - 1 :]
-        for peer in plane_cross:
-            send(group + 3, tops_send.at[step], tops_recv.at[step, slot], peer)
+        for peer in plane_next:
+            send(
+                15 + step,
+                tops_send.at[step, SWEEPS],
+                tops_recv.at[step, slot, SWEEPS],
+                peer,
+            )
         padded[8 : BL + 8, :] = iterate
         own, other = frames()
         near_send[step] = other
@@ -426,7 +444,8 @@
                             still_all[h, m, side, 2 * k : 2 * k + 2, :] = still_recv[
                                 2 * k + h, m, side
                             ]
-        arrived(group + 3, tops_recv.at[step, 0 : 2 * K - 1])
+        arrived(group + 3, tops_recv.at[step, 0 : 2 * K - 1, 0:SWEEPS])
+        arrived(15 + step, tops_recv.at[step, 0 : len(plane_next), SWEEPS])
         for k in range(K):
             for j in range(SWEEPS + 1):
                 for h in range(2):
@@ -579,7 +598,7 @@
         in_specs=[pl.BlockSpec(memory_space=pltpu.HBM)] * 8,
         out_specs=(vmem, vmem),
         scratch_shapes=[pltpu.VMEM(shape, dtype) for shape, dtype in shapes]
-        + [pltpu.SemaphoreType.DMA((n,)) for n in (15, 15, 8)],
+        + [pltpu.SemaphoreType.DMA((n,)) for n in (17, 17, 8)],
         compiler_params=pltpu.CompilerParams(collective_id=0, has_side_effects=True),
         name="adi",
     )(

time: 72.6 us -> 72 us (level)
  no operation moved by 1% of the time
where the time goes in v7:
time: 72 us; the launch traced here: 71.8 us
  Pallas kernels  71.1 us (99%)
    pallas_call x1, Pallas kernels, diffuse(): pl.pallas_call(functools.partial(adi_kernel, (K, Q, C, RD, NC, BL)), out_...  69.7 us

profile of v7, /device:TPU:1, one launch (start us, length us, event | category | flops | bytes accessed | tf_op | source)
XLA Modules:
  0.0 71.8 jit_solution(2689844929203290748)
XLA Ops:
  0.6 69.7 %adi.1 = (f32[4,640]{1,0:T(4,128)}, f32[2,4096]{1,0:T(2,128)}) custom-call(s32[32,128]{1,0:T(8,128)} %bitcast.3, s32[32,128]{1,0:T(8,128)} %bitcast.4, f32[2,4096]{1,0:T(2,128)} %fracs_hbm.1, f32[32,128]{1,0:T(8,128)} %bitcast.5, s32[4,640]{1,0:T(4,128)} %cap_hbm.1, f32[4,640]{1,0:T(4,128)} %blk_hbm.1, f32[5,128,128]{2,1,0:T(8,128)} %rowb_hbm.1, ...), custom_call_target="tpu_custom_call" | custom-call | tf_op jit(solution)/shard_map/adi/pallas_call | solution.py:592
  70.4 1.4 %hand_over.1 = (f32[4,640]{1,0:T(4,128)}, f32[2,4096]{1,0:T(2,128)}) custom-call(f32[4,640]{1,0:T(4,128)} %get-tuple-element.4.first, f32[2,4096]{1,0:T(2,128)} %get-tuple-element.5.second), custom_call_target="tpu_custom_call" | custom-call | tf_op jit(solution)/shard_map/hand_over/pallas_call | solution.py:614

commit v8 on v7

--- a/solution.py
+++ b/solution.py
@@ -176,7 +176,7 @@
                 (cap_hbm, cap_ref),
                 (blk_hbm, blk_ref),
                 (rowb_hbm, rowb_ref),
-                (colb_hbm.at[plane], colb_ref),
+                (colb_hbm, colb_ref),
             )
         )
     ]
@@ -246,7 +246,7 @@
     for n in range(rowb_ref.shape[0]):
         high, low = exact_parts(rowb_ref[n])
         rowb_parts[n] = jnp.concatenate([high, high, low], axis=1)
-    high, low = exact_parts(colb_ref[...])
+    high, low = exact_parts(colb_ref[plane])
     colb_parts[...] = jnp.concatenate([high, high, low], axis=1)
 
     end = lax.broadcasted_iota(jnp.int32, (RD, HC), 1)
@@ -369,7 +369,7 @@
             padded[BL + 8 :, :] = jnp.zeros((8, HC), f32)
             for side, column in ((0, 0), (1, BL - 1)):
                 answer = coupling * jnp.broadcast_to(
-                    colb_ref[:, column : column + 1], (BL, HC)
+                    colb_ref[plane][:, column : column + 1], (BL, HC)
                 )
                 for m in range(SWEEPS):
                     if m > 0:
@@ -378,13 +378,16 @@
                     padded[8 : BL + 8, :] = answer
                     own, other = frames()
                     answer_near[half, m, side] = own
-                    answer_send[m, side] = other
-                    still_send[m, side, 0:1, :] = answer[:1]
-                    still_send[m, side, 1:2, :] = answer[BL - 1 :]
+                    if m == 0:
+                        answer_near[1 - half, m, side] = own
+                    else:
+                        answer_send[m - 1, side] = other
+                        still_send[m - 1, side, 0:1, :] = answer[:1]
+                        still_send[m - 1, side, 1:2, :] = answer[BL - 1 :]
             still_recv[slot] = still_send[...]
             for peer in plane_cross:
                 send(5, still_send, still_recv.at[slot], peer)
-            send(9, answer_send, answer_near.at[half], partner)
+            send(9, answer_send, answer_near.at[half, 1:SWEEPS], partner)
         else:
 
             def prepare(i, carry):
@@ -435,14 +438,21 @@
         tops_recv[step, slot] = tops_send[step]
 
         if step == 0:
+            for k in range(K):
+                for side, column in ((0, 0), (1, BL - 1)):
+                    for t, line in ((0, 0), (1, BL - 1)):
+                        corner = coupling * colb_ref[k][line : line + 1, column : column + 1]
+                        corner = jnp.broadcast_to(corner, (1, HC))
+                        for h in range(2):
+                            still_all[h, 0, side, 2 * k + t : 2 * k + t + 1, :] = corner
             arrived(5, still_recv.at[0 : 2 * K - 1])
-            arrived(9, answer_near.at[0])
+            arrived(9, answer_near.at[0, 1:SWEEPS])
             for k in range(K):
-                for m in range(SWEEPS):
-                    for side in range(2):
-                        for h in range(2):
+                for side in range(2):
+                    for h in range(2):
+                        for m in range(1, SWEEPS):
                             still_all[h, m, side, 2 * k : 2 * k + 2, :] = still_recv[
-                                2 * k + h, m, side
+                                2 * k + h, m - 1, side
                             ]
         arrived(group + 3, tops_recv.at[step, 0 : 2 * K - 1, 0:SWEEPS])
         arrived(15 + step, tops_recv.at[step, 0 : len(plane_next), SWEEPS])
@@ -553,7 +563,7 @@
         ((RD, NC), jnp.int32),
         ((RD, NC), f32),
         ((NB, 128, 128), f32),
-        ((BL, BL), f32),
+        ((K, BL, BL), f32),
         ((bins, 128), f32),
         ((C, RD, NC), f32),
         ((chunks // 2, 128, 256), bf16),
@@ -575,12 +585,12 @@
         ((STEPS, Q, RD, HC), f32),
         ((BL, HC), f32),
         ((BL + 16, HC), f32),
-        ((SWEEPS, 2, 8, HC), f32),
+        ((SWEEPS - 1, 2, 8, HC), f32),
         ((2, SWEEPS, 2, 8, HC), f32),
         ((STEPS, 8, HC), f32),
         ((STEPS, 2, 8, HC), f32),
-        ((SWEEPS, 2, 2, HC), f32),
-        ((2 * K, SWEEPS, 2, 2, HC), f32),
+        ((SWEEPS - 1, 2, 2, HC), f32),
+        ((2 * K, SWEEPS - 1, 2, 2, HC), f32),
         ((2, SWEEPS, 2, 2 * K, HC), f32),
         ((STEPS, SWEEPS + 1, 2, HC), f32),
         ((STEPS, 2 * K, SWEEPS + 1, 2, HC), f32),

time: 72 us -> 72 us (level)
  no operation moved by 1% of the time
where the time goes in v8:
time: 72 us; the launch traced here: 71.8 us
  Pallas kernels  71.1 us (99%)
    pallas_call x1, Pallas kernels, diffuse(): pl.pallas_call(functools.partial(adi_kernel, (K, Q, C, RD, NC, BL)), out_...  69.7 us

profile of v8, /device:TPU:1, one launch (start us, length us, event | category | flops | bytes accessed | tf_op | source)
XLA Modules:
  0.0 71.8 jit_solution(4811463660313884354)
XLA Ops:
  0.6 69.7 %adi.1 = (f32[4,640]{1,0:T(4,128)}, f32[2,4096]{1,0:T(2,128)}) custom-call(s32[32,128]{1,0:T(8,128)} %bitcast.3, s32[32,128]{1,0:T(8,128)} %bitcast.4, f32[2,4096]{1,0:T(2,128)} %fracs_hbm.1, f32[32,128]{1,0:T(8,128)} %bitcast.5, s32[4,640]{1,0:T(4,128)} %cap_hbm.1, f32[4,640]{1,0:T(4,128)} %blk_hbm.1, f32[5,128,128]{2,1,0:T(8,128)} %rowb_hbm.1, ...), custom_call_target="tpu_custom_call" | custom-call | tf_op jit(solution)/shard_map/adi/pallas_call | solution.py:602
  70.4 1.4 %hand_over.1 = (f32[4,640]{1,0:T(4,128)}, f32[2,4096]{1,0:T(2,128)}) custom-call(f32[4,640]{1,0:T(4,128)} %get-tuple-element.4.first, f32[2,4096]{1,0:T(2,128)} %get-tuple-element.5.second), custom_call_target="tpu_custom_call" | custom-call | tf_op jit(solution)/shard_map/hand_over/pallas_call | solution.py:624

commit v9 on v8

--- a/solution.py
+++ b/solution.py
@@ -387,7 +387,6 @@
             still_recv[slot] = still_send[...]
             for peer in plane_cross:
                 send(5, still_send, still_recv.at[slot], peer)
-            send(9, answer_send, answer_near.at[half, 1:SWEEPS], partner)
         else:
 
             def prepare(i, carry):
@@ -402,6 +401,8 @@
             lax.fori_loop(0, chunks // 2, prepare, 0)
 
         arrived(group + 2, field_plane.at[step, 0 : Q - 1])
+        if step == 0:
+            send(9, answer_send, answer_near.at[half, 1:SWEEPS], partner)
         for i in range(Q):
             field_block[RD * i : RD * (i + 1), :] = field_plane[step, i]
 

time: 72 us -> 72.3 us (level)
  no operation moved by 1% of the time
where the time goes in v9:
time: 72.3 us; the launch traced here: 72.1 us
  Pallas kernels  71.4 us (99%)
    pallas_call x1, Pallas kernels, diffuse(): pl.pallas_call(functools.partial(adi_kernel, (K, Q, C, RD, NC, BL)), out_...  70 us

profile of v9, /device:TPU:1, one launch (start us, length us, event | category | flops | bytes accessed | tf_op | source)
XLA Modules:
  0.0 72.1 jit_solution(6286977819055118315)
XLA Ops:
  0.6 70.0 %adi.1 = (f32[4,640]{1,0:T(4,128)}, f32[2,4096]{1,0:T(2,128)}) custom-call(s32[32,128]{1,0:T(8,128)} %bitcast.3, s32[32,128]{1,0:T(8,128)} %bitcast.4, f32[2,4096]{1,0:T(2,128)} %fracs_hbm.1, f32[32,128]{1,0:T(8,128)} %bitcast.5, s32[4,640]{1,0:T(4,128)} %cap_hbm.1, f32[4,640]{1,0:T(4,128)} %blk_hbm.1, f32[5,128,128]{2,1,0:T(8,128)} %rowb_hbm.1, ...), custom_call_target="tpu_custom_call" | custom-call | tf_op jit(solution)/shard_map/adi/pallas_call | solution.py:603
  70.7 1.4 %hand_over.1 = (f32[4,640]{1,0:T(4,128)}, f32[2,4096]{1,0:T(2,128)}) custom-call(f32[4,640]{1,0:T(4,128)} %get-tuple-element.4.first, f32[2,4096]{1,0:T(2,128)} %get-tuple-element.5.second), custom_call_target="tpu_custom_call" | custom-call | tf_op jit(solution)/shard_map/hand_over/pallas_call | solution.py:625
